TPU v7x, 256 devices: a whole 4x4x8 slice. The times are simulated.
256 devices in a mesh: rows: 32 (over z, y), cols: 8 (over x, core).
Axes of the slice: x: 4, y: 4, z: 8, core: 2. Of those that a mesh axis runs over, the one named last changes fastest.
Arguments:
- matrix: float32 [32768, 10, 1024], P('rows', None, 'cols'), may hold values from -6 to 6
Outputs:
- reduced: float32 [32768, 10, 1024], P('rows', None, 'cols')
- top_rows: float32 [256, 10, 1024], P(None, None, 'cols')
All inputs are finite; a program needn't handle non-finite values.
Results may differ from a plain program's by a relative error of at most 0.0001.
Values sent between devices are 32-bit elements; how exact they have to be, the bound alone decides.
No kernel may reach another device: no remote copies, remote signals or barrier semaphores. Data moves between devices by JAX's collectives and lax.ppermute only.
A program may use at most 64 MiB of HBM per device.

v0:
```python
import jax
import jax.numpy as jnp
from jax import lax
from jax.sharding import PartitionSpec as P

PRECISE = lax.Precision.HIGHEST


def spread(block, axis, owner):
    block = jnp.where(lax.axis_index(axis) == owner, block, jnp.zeros_like(block))
    return lax.psum(block, axis)


def product(left, right):
    return jnp.dot(left, right, precision=PRECISE, preferred_element_type=jnp.float32)


def relay_panel(panel_block, root_index):
    return spread(panel_block, "cols", root_index)


def factor(panel, columns):
    gram_block = product(panel.T, panel)
    cross_terms = product(panel.T, columns)
    gram_block, cross_terms = lax.psum((gram_block, cross_terms), "rows")
    triangle = jnp.linalg.cholesky(gram_block)
    weights = jax.scipy.linalg.solve_triangular(triangle, cross_terms, lower=True)
    coefficients = jax.scipy.linalg.solve_triangular(triangle, weights, trans=1, lower=True)
    return (weights, columns - product(panel, coefficients))


def shards(matrix):
    rows_dev, rounds, width = matrix.shape
    columns = matrix.reshape(rows_dev, rounds * width)
    first_panel = relay_panel(columns[:, :width], 0)
    first_rows, columns = factor(first_panel, columns)
    second_panel = relay_panel(columns[:, :width], 1)
    second_rows, columns = factor(second_panel, columns)
    triangle_rows = jnp.concatenate([first_rows, second_rows], axis=0)
    return (
        columns.reshape(rows_dev, rounds, width),
        triangle_rows.reshape(2 * width, rounds, width),
    )


def solution(mesh):
    placed = (P("rows", None, "cols"),)
    return jax.shard_map(
        shards,
        mesh=mesh,
        in_specs=placed,
        out_specs=(P("rows", None, "cols"), P(None, None, "cols")),
        check_vma=False,
    )
```

profile of v0, /device:TPU:8, one launch (start us, length us, event | category | flops | bytes accessed | tf_op | source)
XLA Modules:
  0.0 560.7 jit_solution(4598258446387686267)
XLA Ops:
  7.2 0.0 all-reduce.7.cloned.1.call-start
  7.2 5.9 %copy.10 = f32[1024,10,128]{0,2,1:T(8,128)} copy(f32[1024,10,128]{2,0,1:T(8,128)} %param.6) | data formatting | bytes 10485760 | tf_op args[0]
  13.1 5.9 %copy.14 = f32[1024,1280]{1,0:T(8,128)} copy(f32[1024,1280]{0,1:T(8,128)} %bitcast.45) | data formatting | bytes 10485760 | tf_op jit(solution)/shard_map/reshape | solution.py:34
  19.0 1.9 slice_select_fusion.1
  20.9 0.0 all-reduce.7.cloned.1.call-update
  20.9 0.0 all-reduce.13.cloned.1.call-start
  21.0 68.7 %all-reduce.7.cloned.1.call-done = f32[1024,128]{1,0:T(8,128)} async-done(((f32[1024,128]{1,0:T(8,128)}), f32[1024,128]{1,0:T(8,128)}) %all-reduce.7.cloned.1.call-update) | async-done | bytes 524304 | tf_op jit(solution)/shard_map/psum | solution.py:11
  89.7 0.0 copy-start.1
  89.7 8.0 %fusion.13 = f32[128,1280]{1,0:T(8,128)} fusion(f32[1024,128]{1,0:T(8,128)} %all-reduce.7.cloned.1.call-done, f32[1024,1280]{0,1:T(8,128)} %bitcast.46), kind=kOutput, calls=%fused_computation.28 | convolution fusion | flops 2013265920 | bytes 6422528 | tf_op jit(solution)/shard_map/dot_general | solution.py:15
  97.7 0.0 copy-done.1
  97.7 1.6 fusion.12
  99.3 0.0 all-reduce.13.cloned.1.call-update
  99.3 0.2 all-reduce.9.cloned.1.call-start
  99.5 146.6 %all-reduce.13.cloned.1.call-done = (f32[128,1280]{1,0:T(8,128)}, f32[128,128]{0,1:T(8,128)}) async-done(((f32[128,1280]{1,0:T(8,128)}, f32[128,128]{0,1:T(8,128)}), (f32[128,1280]{1,0:T(8,128)}, f32[128,128]{0,1:T(8,128)})) %all-reduce.13.cloned.1.call-update) | async-done | bytes 720912 | tf_op jit(solution)/shard_map/psum | solution.py:25
  246.1 0.9 copy.13
  247.1 0.9 fusion.11
  247.9 11.7 %cholesky.44 = f32[128,128]{1,0:T(8,128)S(1)} custom-call(f32[128,128]{1,0:T(8,128)S(1)} %fusion.11), custom_call_target="Cholesky" | custom-call | tf_op jit(solution)/shard_map/jit(cholesky)/cholesky | solution.py:26
  259.7 0.6 compare_reduce_fusion.1
  260.3 0.7 fusion
  261.0 9.8 %custom-call.11 = f32[1,128,128]{1,2,0:T(8,128)S(1)} custom-call(f32[1,128,128]{2,1,0:T(8,128)S(1)} %fusion), custom_call_target="InvertDiagBlocksLowerTriangular" | custom-call | tf_op jit(solution)/shard_map/jit(_solve_triangular)/triangular_solve | solution.py:28
  270.8 1.8 fusion.7
  272.6 0.7 fusion.9
  273.3 6.4 %convolution_subtract_fusion.1 = f32[1024,1280]{1,0:T(8,128)S(1)} fusion(f32[1024,1280]{1,0:T(8,128)} %copy.14, f32[1024,128]{1,0:T(8,128)S(1)} %copy-done.1, f32[128,1280]{1,0:T(8,128)S(1)} %fusion.9), kind=kOutput, calls=%fused_computation.1 | convolution fusion | flops 2014576640 | bytes 11665408 | tf_op jit(solution)/shard_map/dot_general | solution.py:15
  279.7 0.0 copy-start
  279.7 2.3 copy-done
  282.0 0.8 slice_select_fusion
  282.9 0.0 all-reduce.9.cloned.1.call-update
  282.9 0.3 all-reduce.11.cloned.1.call-start
  283.2 63.7 %all-reduce.9.cloned.1.call-done = f32[1024,128]{1,0:T(8,128)} async-done(((f32[1024,128]{1,0:T(8,128)}), f32[1024,128]{1,0:T(8,128)}) %all-reduce.9.cloned.1.call-update) | async-done | bytes 524304 | tf_op jit(solution)/shard_map/psum | solution.py:11
  346.9 2.9 fusion.14
  349.7 0.0 copy-start.2
  349.7 6.3 %fusion.15 = f32[128,1280]{1,0:T(8,128)} fusion(f32[1024,128]{1,0:T(8,128)} %all-reduce.9.cloned.1.call-done, f32[1024,1280]{1,0:T(8,128)} %copy-done), kind=kOutput, calls=%fused_computation.30 | convolution fusion | flops 2013265920 | bytes 6422528 | tf_op jit(solution)/shard_map/dot_general | solution.py:15
  356.1 0.0 all-reduce.11.cloned.1.call-update
  356.1 146.8 %all-reduce.11.cloned.1.call-done = (f32[128,1280]{1,0:T(8,128)}, f32[128,128]{0,1:T(8,128)}) async-done(((f32[128,1280]{1,0:T(8,128)}, f32[128,128]{0,1:T(8,128)}), (f32[128,1280]{1,0:T(8,128)}, f32[128,128]{0,1:T(8,128)})) %all-reduce.11.cloned.1.call-update) | async-done | bytes 720912 | tf_op jit(solution)/shard_map/psum | solution.py:25
  502.9 0.9 copy.16
  503.8 0.9 fusion.6
  504.7 11.7 %cholesky.55 = f32[128,128]{1,0:T(8,128)S(1)} custom-call(f32[128,128]{1,0:T(8,128)S(1)} %fusion.6), custom_call_target="Cholesky" | custom-call | tf_op jit(solution)/shard_map/jit(cholesky)/cholesky | solution.py:26
  516.4 0.6 compare_reduce_fusion
  517.1 0.7 fusion.1
  517.8 9.8 %custom-call.13 = f32[1,128,128]{1,2,0:T(8,128)S(1)} custom-call(f32[1,128,128]{2,1,0:T(8,128)S(1)} %fusion.1), custom_call_target="InvertDiagBlocksLowerTriangular" | custom-call | tf_op jit(solution)/shard_map/jit(_solve_triangular)/triangular_solve | solution.py:28
  527.6 1.8 fusion.2
  529.4 0.7 fusion.4
  530.1 0.1 pad_maximum_fusion
  530.2 0.0 copy-done.2
  530.2 7.9 %convolution_subtract_fusion = f32[1024,1280]{1,0:T(8,128)} fusion(f32[1024,1280]{1,0:T(8,128)} %copy-done, f32[1024,128]{1,0:T(8,128)S(1)} %copy-done.2, f32[128,1280]{1,0:T(8,128)S(1)} %fusion.4), kind=kOutput, calls=%fused_computation | convolution fusion | flops 2014576640 | bytes 11665408 | tf_op jit(solution)/shard_map/dot_general | solution.py:15
  538.1 5.9 %copy.17 = f32[1024,1280]{0,1:T(8,128)} copy(f32[1024,1280]{1,0:T(8,128)} %convolution_subtract_fusion) | data formatting | bytes 10485760 | tf_op jit(solution)/shard_map/sub | solution.py:29
  544.0 5.9 %copy.19 = f32[1024,10,128]{2,0,1:T(8,128)} copy(f32[1024,10,128]{0,2,1:T(8,128)} %bitcast.47) | data formatting | bytes 10485760
  549.9 1.5 copy.18
  551.4 2.8 copy.20
  (2 shorter events, 0.1 us)
Async XLA Ops:
  7.2 82.5 %all-reduce.7.cloned.1.call-start = ((), (), s32[]{:S(2)}) async-start(), calls=%async_computation | async-start | bytes 1048576 | tf_op jit(solution)/shard_map/psum | solution.py:11
  20.9 225.2 %all-reduce.13.cloned.1.call-start = ((), (), s32[]{:S(2)}) async-start(), calls=%async_computation.3 | async-start | bytes 1441792 | tf_op jit(solution)/shard_map/psum | solution.py:25
  89.7 8.0 %copy-start.1 = (f32[1024,128]{1,0:T(8,128)S(1)}, f32[1024,128]{1,0:T(8,128)}, u32[]{:S(2)}) copy-start(f32[1024,128]{1,0:T(8,128)} %all-reduce.7.cloned.1.call-done) | copy-start | bytes 1572868
  99.3 247.6 %all-reduce.9.cloned.1.call-start = ((), (), s32[]{:S(2)}) async-start(), calls=%async_computation.1 | async-start | bytes 1048576 | tf_op jit(solution)/shard_map/psum | solution.py:11
  279.7 2.4 copy-start
  282.9 220.0 %all-reduce.11.cloned.1.call-start = ((), (), s32[]{:S(2)}) async-start(), calls=%async_computation.2 | async-start | bytes 1441792 | tf_op jit(solution)/shard_map/psum | solution.py:25
  349.7 180.4 %copy-start.2 = (f32[1024,128]{1,0:T(8,128)S(1)}, f32[1024,128]{1,0:T(8,128)}, u32[]{:S(2)}) copy-start(f32[1024,128]{1,0:T(8,128)} %all-reduce.9.cloned.1.call-done) | copy-start | bytes 1572868
Sparse Core Ops, SparseCore 0:
  21.1 68.5 all-reduce.6
  99.4 146.6 all-reduce.12
  283.0 63.8 all-reduce.8
  356.2 146.6 all-reduce.10
where the time goes:
time: 563 us; the launch traced here: 561 us
  waiting for transfers between devices  426 us (76%)
  other arithmetic  50.2 us (9%)
  matrix products  38.1 us (7%)
  local copies, waits for them, and re-layouts  32.1 us (6%)
  between operations  13.9 us (2%)
    psum x2, waiting for transfers between devices, factor(): gram_block, cross_terms = lax.psum((gram_block, cross_terms), 'rows')  293 us
    psum x2, waiting for transfers between devices, spread(): return lax.psum(block, axis)  132 us
    dot_general x6, matrix products, product(): jnp.dot(left, right, precision=PRECISE, preferred_element_type=jnp.float32)  33.1 us
    another operation x6, other arithmetic, factor(): triangle = jnp.linalg.cholesky(gram_block)  24.8 us
    another operation x4, other arithmetic, factor(): jax.scipy.linalg.solve_triangular(triangle, weights, trans=1, lower=True)  20.9 us
    unnamed x9, local copies, waits for them, and re-layouts  16.9 us
  transfers between devices with their start and end apart: 4, of which 4 were waited for; matrix products, arithmetic and copies ran while one was open for 0% of the time, Pallas kernels for 0%

commit v1 on v0

v1 whole, which is shorter than its diff:
```python
import functools

import jax
import jax.numpy as jnp
from jax import lax
from jax.experimental import pallas as pl
from jax.experimental.pallas import tpu as pltpu
from jax.sharding import Mesh, PartitionSpec as P

PRECISE = lax.Precision.HIGHEST
NZ, NY, NX, NC = 8, 4, 4, 2


def dot(left, right, dims=(((1,), (0,)), ((), ()))):
    return lax.dot_general(left, right, dims, precision=PRECISE, preferred_element_type=jnp.float32)


def relay(own):
    x = lax.axis_index("x")
    half = own.shape[0] // 2
    low, high = own[:half], own[half:]
    up = [(0, 1)]
    down = [(0, 3)]
    s_up = lax.ppermute(low, "x", up)
    s_down = lax.ppermute(high, "x", down)
    t_up = lax.ppermute(jnp.where(x == 0, high, s_up), "x", [(0, 1), (1, 2)])
    t_down = lax.ppermute(jnp.where(x == 0, low, s_down), "x", [(0, 3), (3, 2)])
    got_low = jnp.where(x == 0, low, jnp.where(x == 1, s_up, jnp.where(x == 2, t_up, t_down)))
    got_high = jnp.where(x == 0, high, jnp.where(x == 1, t_up, jnp.where(x == 2, t_down, s_down)))
    mine = jnp.concatenate([got_low, got_high], axis=0)
    other = lax.ppermute(mine, "c", [(0, 1), (1, 0)])
    core = lax.axis_index("c")
    first = jnp.where(core == 0, mine, other)
    second = jnp.where(core == 0, other, mine)
    return jnp.concatenate([first, second], axis=1)


def gram_kernel(p_ref, g_ref):
    p = p_ref[...]
    g_ref[...] = dot(p.T, p)


def gram_of(panels):
    n, w = panels.shape
    return pl.pallas_call(
        gram_kernel,
        out_shape=jax.ShapeDtypeStruct((w, w), jnp.float32),
        name="gram",
    )(panels)


def cross_kernel(p_ref, c_ref, o_ref, pt_ref):
    @pl.when(pl.program_id(0) == 0)
    def _():
        pt_ref[...] = p_ref[...].T

    pair = jnp.concatenate([c_ref[0], c_ref[1]], axis=1)
    o_ref[...] = dot(pt_ref[...], pair)


def cross_of(panels, columns):
    rounds, n, k = columns.shape
    w = panels.shape[1]
    return pl.pallas_call(
        cross_kernel,
        grid=(rounds // 2,),
        in_specs=[
            pl.BlockSpec((n, w), lambda i: (0, 0)),
            pl.BlockSpec((2, n, k), lambda i: (i, 0, 0)),
        ],
        out_specs=pl.BlockSpec((w, 2 * k), lambda i: (0, i)),
        out_shape=jax.ShapeDtypeStruct((w, rounds * k), jnp.float32),
        scratch_shapes=[pltpu.VMEM((w, n), jnp.float32)],
        name="cross",
    )(panels, columns)


def update_kernel(w_ref, x_ref, p_ref, c_ref, red_ref, top_ref):
    inverse = w_ref[...]
    top = dot(inverse, x_ref[...])
    k = c_ref.shape[2]
    top_ref[0] = top[:, :k]
    top_ref[1] = top[:, k:]
    coefficients = dot(inverse.T, top)
    fit = dot(p_ref[...], coefficients)
    red_ref[0] = c_ref[0] - fit[:, :k]
    red_ref[1] = c_ref[1] - fit[:, k:]


def update(inverse, cross, panels, columns):
    rounds, n, k = columns.shape
    w = panels.shape[1]
    return pl.pallas_call(
        update_kernel,
        grid=(rounds // 2,),
        in_specs=[
            pl.BlockSpec((w, w), lambda i: (0, 0)),
            pl.BlockSpec((w, 2 * k), lambda i: (0, i)),
            pl.BlockSpec((n, w), lambda i: (0, 0)),
            pl.BlockSpec((2, n, k), lambda i: (i, 0, 0)),
        ],
        out_specs=[
            pl.BlockSpec((2, n, k), lambda i: (i, 0, 0)),
            pl.BlockSpec((2, w, k), lambda i: (i, 0, 0)),
        ],
        out_shape=[
            jax.ShapeDtypeStruct((rounds, n, k), jnp.float32),
            jax.ShapeDtypeStruct((rounds, w, k), jnp.float32),
        ],
        compiler_params=pltpu.CompilerParams(vmem_limit_bytes=48 << 20),
        name="update",
    )(inverse, cross, panels, columns)


def scatter_sum(values, axis, parts):
    rows, width = values.shape
    pieces = lax.all_to_all(values.reshape(parts, rows // parts, width), axis, 0, 0)
    return jnp.sum(pieces, axis=0)


def gather(values, axis, parts):
    rows, width = values.shape
    copies = jnp.broadcast_to(values[None], (parts, rows, width))
    return lax.all_to_all(copies, axis, 0, 0).reshape(parts * rows, width)


def reduce_rows(values):
    part = scatter_sum(values, "y", NY)
    part = scatter_sum(part, "z", NZ)
    part = gather(part, "z", NZ)
    return gather(part, "y", NY)


def shards(matrix):
    columns = jnp.transpose(matrix, (1, 0, 2))
    panels = relay(columns[0])
    gram = reduce_rows(gram_of(panels))
    cross = reduce_rows(cross_of(panels, columns))
    triangle = jnp.linalg.cholesky(gram)
    eye = jnp.eye(gram.shape[0], dtype=jnp.float32)
    inverse = jax.scipy.linalg.solve_triangular(triangle, eye, lower=True)
    reduced, top = update(inverse, cross, panels, columns)
    return jnp.transpose(reduced, (1, 0, 2)), jnp.transpose(top, (1, 0, 2))


def solution(mesh):
    fine = Mesh(mesh.devices.reshape(NZ, NY, NX, NC), ("z", "y", "x", "c"))
    return jax.shard_map(
        shards,
        mesh=fine,
        in_specs=(P(("z", "y"), None, ("x", "c")),),
        out_specs=(P(("z", "y"), None, ("x", "c")), P(None, None, ("x", "c"))),
        check_vma=False,
    )
```

time: 563 us -> 192 us (0.34)
  waiting for transfers between devices: 426 us -> 21.8 us
  blocking collectives: 0 us -> 37.8 us
  matrix products: 38.1 us -> 1.31 us
  starting transfers between devices: 0.57 us -> 37 us
  local copies, waits for them, and re-layouts: 32.1 us -> 7.79 us
  Pallas kernels: 0 us -> 24.3 us
  between operations: 13.9 us -> 2.11 us
  other arithmetic: 50.2 us -> 58 us
    psum x4 -> x0, waiting for transfers between devices: 426 us -> none  [the longest x2 293 us: factor(): gram_block, cross_terms = lax.psum((gram_block, cross_terms), 'rows')]
    all_to_all x0 -> x3, blocking collectives: none -> 37.8 us  [the longest x2 27.1 us: scatter_sum(): lax.all_to_all(values.reshape(parts, rows // parts, width), axis, 0, 0)]
    dot_general x6 -> x0, matrix products: 33.1 us -> none  [product(): jnp.dot(left, right, precision=PRECISE, preferred_element_type=jnp.float32)]
    all_to_all x0 -> x5, starting transfers between devices: none -> 25.3 us  [the longest x3 16.7 us: gather(): return lax.all_to_all(copies, axis, 0, 0).reshape(parts * rows, width)]
    pallas_call x0 -> x3, Pallas kernels: none -> 24.3 us  [the longest x1 12.6 us: update(): pl.pallas_call(update_kernel, grid=(rounds // 2,), in_specs=[pl.BlockSpec...]
    unnamed x9 -> x2, local copies, waits for them, and re-layouts: 16.9 us -> 0.01 us
    ppermute x0 -> x5, waiting for transfers between devices: none -> 12.1 us  [the longest x1 4.21 us: relay(): s_down = lax.ppermute(high, 'x', down)]
    ppermute x0 -> x5, starting transfers between devices: none -> 11.7 us  [the longest x1 4.68 us: relay(): s_down = lax.ppermute(high, 'x', down)]
  transfers between devices with their start and end apart: 4 -> 10, of which waited for: 4 -> 7; matrix products, arithmetic and copies ran while one was open for 0% -> 31% of each run, Pallas kernels for 0% -> 5%
where the time goes in v1:
time: 192 us; the launch traced here: 190 us
  other arithmetic  58 us (30%)
  blocking collectives  37.8 us (20%)
  starting transfers between devices  37 us (19%)
  Pallas kernels  24.3 us (13%)
  waiting for transfers between devices  21.8 us (11%)
  local copies, waits for them, and re-layouts  7.79 us (4%)
  between operations  2.11 us (1%)
    another operation x6, other arithmetic, shards(): triangle = jnp.linalg.cholesky(gram)  34 us
    all_to_all x2, blocking collectives, scatter_sum(): lax.all_to_all(values.reshape(parts, rows // parts, width), axis, 0, 0)  27.1 us
    another operation x4, other arithmetic, shards(): inverse = jax.scipy.linalg.solve_triangular(triangle, eye, lower=True)  19.7 us
    all_to_all x3, starting transfers between devices, gather(): return lax.all_to_all(copies, axis, 0, 0).reshape(parts * rows, width)  16.7 us
    pallas_call x1, Pallas kernels, update(): pl.pallas_call(update_kernel, grid=(rounds // 2,), in_specs=[pl.BlockSpec...  12.6 us
    all_to_all x1, blocking collectives, gather(): return lax.all_to_all(copies, axis, 0, 0).reshape(parts * rows, width)  10.8 us
    all_to_all x3, waiting for transfers between devices, gather(): return lax.all_to_all(copies, axis, 0, 0).reshape(parts * rows, width)  9.22 us
    pallas_call x1, Pallas kernels, cross_of(): pl.pallas_call(cross_kernel, grid=(rounds // 2,), in_specs=[pl.BlockSpec(...  8.61 us
  transfers between devices with their start and end apart: 10, of which 7 were waited for; matrix products, arithmetic and copies ran while one was open for 31% of the time, Pallas kernels for 5%

profile of v1, /device:TPU:8, one launch (start us, length us, event | category | flops | bytes accessed | tf_op | source)
XLA Modules:
  0.0 190.0 jit_solution(3526136643571559297)
XLA Ops:
  0.6 1.1 slice_bitcast_fusion
  1.7 4.7 %collective-permute-start.2 = (f32[512,128]{1,0:T(8,128)S(1)}, f32[512,128]{1,0:T(8,128)S(1)}, u32[]{:S(2)}, u32[]{:S(2)}) collective-permute-start(f32[512,128]{1,0:T(8,128)S(1)} %get-tuple-element.28), channel_id=1, source_target_pairs={{0,6},{1,7},{8,14},{9,15},{16,22},{17,23},{24,30},{25,31},{32,38},... | collective-permute-start | bytes 786440 | tf_op jit(solution)/shard_map/ppermute | solution.py:25
  6.4 1.3 collective-permute-start
  7.7 4.2 %collective-permute-done.2 = f32[512,128]{1,0:T(8,128)S(1)} collective-permute-done((f32[512,128]{1,0:T(8,128)S(1)}, f32[512,128]{1,0:T(8,128)S(1)}, u32[]{:S(2)}, u32[]{:S(2)}) %collective-permute-start.2) | collective-permute-done | bytes 262176 | tf_op jit(solution)/shard_map/ppermute | solution.py:25
  11.9 1.3 collective-permute-done
  13.2 1.1 broadcast_select_fusion.2
  14.3 4.3 %collective-permute-start.3 = (f32[512,128]{1,0:T(8,128)S(1)}, f32[512,128]{1,0:T(8,128)S(1)}, u32[]{:S(2)}, u32[]{:S(2)}) collective-permute-start(f32[512,128]{1,0:T(8,128)S(1)} %get-tuple-element.26), channel_id=1, source_target_pairs={{0,6},{6,4},{1,7},{7,5},{8,14},{14,12},{9,15},{15,13},{16,22},{22,... | collective-permute-start | bytes 786440 | tf_op jit(solution)/shard_map/ppermute | solution.py:27
  18.6 1.3 collective-permute-start.1
  19.9 3.3 %collective-permute-done.3 = f32[512,128]{1,0:T(8,128)S(1)} collective-permute-done((f32[512,128]{1,0:T(8,128)S(1)}, f32[512,128]{1,0:T(8,128)S(1)}, u32[]{:S(2)}, u32[]{:S(2)}) %collective-permute-start.3) | collective-permute-done | bytes 262176 | tf_op jit(solution)/shard_map/ppermute | solution.py:27
  23.3 1.3 collective-permute-done.1
  24.6 1.1 select_select_fusion.2
  25.8 0.1 collective-permute-start.4
  25.9 1.9 collective-permute-done.4
  27.7 0.1 broadcast_select_fusion.1
  27.8 1.0 pad_maximum_fusion.p_ref
  28.9 3.1 %gram.1 = f32[256,256]{1,0:T(8,128)} custom-call(f32[1024,256]{1,0:T(8,128)} %pad_maximum_fusion.p_ref), custom_call_target="tpu_custom_call" | custom-call | tf_op jit(solution)/shard_map/gram/pallas_call | solution.py:45
  32.0 10.4 %all_to_all.40 = f32[4,64,256]{2,1,0:T(8,128)S(1)} all-to-all(f32[4,64,256]{2,1,0:T(8,128)} %bitcast.64), channel_id=1, replica_groups=mesh['z'=8,'y'=4,'x'=4,'c'=2] {'y'}, dimensions={0} | all-to-all | bytes 524288 | tf_op jit(solution)/shard_map/all_to_all | solution.py:117
  42.4 16.6 %all_to_all.41 = f32[8,8,256]{2,1,0:T(8,128)S(1)} all-to-all(f32[8,8,256]{2,1,0:T(8,128)S(1)} %bitcast.65), channel_id=1, replica_groups=mesh['z'=8,'y'=4,'x'=4,'c'=2] {'z'}, dimensions={0} | all-to-all | bytes 131072 | tf_op jit(solution)/shard_map/all_to_all | solution.py:117
  59.1 10.8 %all_to_all.42 = f32[8,8,256]{2,1,0:T(8,128)S(1)} all-to-all(f32[8,8,256]{2,1,0:T(8,128)S(1)} %broadcast_in_dim.13), channel_id=1, replica_groups=mesh['z'=8,'y'=4,'x'=4,'c'=2] {'z'}, dimensions={0} | all-to-all | bytes 131072 | tf_op jit(solution)/shard_map/all_to_all | solution.py:124
  69.8 0.7 broadcast_in_dim.30
  70.5 4.8 %all-to-all-start.3 = ((f32[4,64,256]{2,1,0:T(8,128)}), f32[4,64,256]{2,1,0:T(8,128)S(1)}, u32[]{:S(2)}, u32[]{:S(2)}) async-start(f32[4,64,256]{2,1,0:T(8,128)} %broadcast_in_dim.30), calls=%async_computation.3 | async-start | bytes 524288 | tf_op jit(solution)/shard_map/all_to_all | solution.py:124
  75.4 8.6 %cross.1 = f32[256,1280]{1,0:T(8,128)} custom-call(f32[1024,256]{1,0:T(8,128)} %pad_maximum_fusion.p_ref, f32[10,1024,128]{2,1,0:T(8,128)} %bitcast.59), custom_call_target="tpu_custom_call" | custom-call | tf_op jit(solution)/shard_map/cross/pallas_call | solution.py:64
  84.0 0.0 all-to-all-done.3
  84.0 4.8 %all-to-all-start.4 = ((f32[4,64,1280]{2,1,0:T(8,128)}), f32[4,64,1280]{2,1,0:T(8,128)S(1)}, u32[]{:S(2)}, u32[]{:S(2)}) async-start(f32[4,64,1280]{2,1,0:T(8,128)} %bitcast.61), calls=%async_computation.4 | async-start | bytes 2621440 | tf_op jit(solution)/shard_map/all_to_all | solution.py:117
  88.8 0.1 copy.5
  89.0 11.7 %cholesky.50 = f32[128,128]{1,0:T(8,128)S(1)} custom-call(f32[128,128]{1,0:T(8,128)S(1)} %cholesky.118), custom_call_target="Cholesky" | custom-call | tf_op jit(solution)/shard_map/jit(cholesky)/cholesky | solution.py:139
  100.8 0.5 all-to-all-done.4
  101.2 0.8 reduce_sum.38
  102.0 0.0 copy-start
  102.0 3.7 %all-to-all-start.5 = ((f32[8,8,1280]{2,1,0:T(8,128)}), f32[8,8,1280]{2,1,0:T(8,128)S(1)}, u32[]{:S(2)}, u32[]{:S(2)}) async-start(f32[8,8,1280]{2,1,0:T(8,128)} %bitcast.13), calls=%async_computation.5 | async-start | bytes 655360 | tf_op jit(solution)/shard_map/all_to_all | solution.py:117
  105.8 9.8 %custom-call.15 = f32[1,128,128]{1,2,0:T(8,128)S(1)} custom-call(f32[1,128,128]{2,1,0:T(8,128)S(1)} %get-tuple-element.35), custom_call_target="InvertDiagBlocksLowerTriangular" | custom-call | tf_op jit(solution)/shard_map/jit(cholesky)/cholesky | solution.py:139
  115.7 0.2 constant_dynamic-update-slice_fusion.1
  115.9 0.3 convolution_subtract_fusion.1
  116.1 11.7 %cholesky.105 = f32[128,128]{1,0:T(8,128)S(1)} custom-call(f32[128,128]{1,0:T(8,128)S(1)} %convolution_subtract_fusion.1), custom_call_target="Cholesky" | custom-call | tf_op jit(solution)/shard_map/jit(cholesky)/cholesky | solution.py:139
  127.8 0.0 all-to-all-done.5
  127.9 0.7 broadcast_in_dim.31
  128.6 6.9 %all-to-all-start.6 = ((f32[8,8,1280]{2,1,0:T(8,128)}), f32[8,8,1280]{2,1,0:T(8,128)S(1)}, u32[]{:S(2)}, u32[]{:S(2)}) async-start(f32[8,8,1280]{2,1,0:T(8,128)} %broadcast_in_dim.31), calls=%async_computation.6 | async-start | bytes 655360 | tf_op jit(solution)/shard_map/all_to_all | solution.py:124
  135.6 0.7 compare_reduce_fusion
  137.5 9.2 %all-to-all-done.6 = f32[8,8,1280]{2,1,0:T(8,128)S(1)} async-done(((f32[8,8,1280]{2,1,0:T(8,128)}), f32[8,8,1280]{2,1,0:T(8,128)S(1)}, u32[]{:S(2)}, u32[]{:S(2)}) %all-to-all-start.6) | async-done | bytes 327712 | tf_op jit(solution)/shard_map/all_to_all | solution.py:124
  146.8 1.2 broadcast_in_dim.33
  147.9 5.0 %all-to-all-start.7 = ((f32[4,64,1280]{2,1,0:T(8,128)}), f32[4,64,1280]{2,1,0:T(8,128)S(1)}, u32[]{:S(2)}, u32[]{:S(2)}) async-start(f32[4,64,1280]{2,1,0:T(8,128)} %broadcast_in_dim.33), calls=%async_computation.7 | async-start | bytes 2621440 | tf_op jit(solution)/shard_map/all_to_all | solution.py:124
  152.9 0.1 triangular_solve.63
  153.0 3.9 %while.1 = (s32[]{:T(128)}, f32[256,256]{1,0:T(8,128)S(1)}, s32[2,2]{1,0:T(2,128)S(1)}, f32[2,128,128]{2,1,0:T(8,128)S(1)}, s32[]{:T(128)}) while((s32[]{:T(128)}, f32[256,256]{1,0:T(8,128)S(1)}, s32[2,2]{1,0:T(2,128)S(1)}, f32[2,128,128]{2,1,0:T(8,128)S(1)}, s32[]{:T(128)}) %tuple.31), condition=%wide.while_cond, body=%wide.while_body.sunk | while | flops 2 | bytes 131189 | solution.py:141
  153.0 0.6 fusion.14
  153.6 1.3 bitcast_dynamic-update-slice_fusion.2
  154.9 0.6 fusion.14
  155.5 1.3 bitcast_dynamic-update-slice_fusion.2
  156.9 19.7 %custom-call.16 = f32[2,128,128]{1,2,0:T(8,128)S(1)} custom-call(f32[2,128,128]{2,1,0:T(8,128)S(1)} %get-tuple-element.13), custom_call_target="InvertDiagBlocksLowerTriangular" | custom-call | tf_op jit(solution)/shard_map/jit(_solve_triangular)/triangular_solve | solution.py:141
  176.6 0.3 fusion.1
  176.8 0.3 convolution_subtract_fusion
  177.1 0.3 fusion.4
  177.4 0.0 all-to-all-done.7
  177.5 0.0 copy-done
  177.5 12.6 %update.1 = (f32[10,1024,128]{2,1,0:T(8,128)}, f32[10,256,128]{2,1,0:T(8,128)}) custom-call(f32[256,256]{1,0:T(8,128)S(1)} %pad_maximum_fusion.2.w_ref, f32[256,1280]{1,0:T(8,128)S(1)} %bitcast.55, f32[1024,256]{1,0:T(8,128)S(1)} %copy-done, f32[10,1024,128]{2,1,0:T(8,128)} %bitcast.60), custom_call_target="tpu_custom_call" | custom-call | tf_op jit(solution)/shard_map/update/pallas_call | solution.py:93
  (17 shorter events, 0.3 us)
Async XLA Ops:
  1.7 10.2 %collective-permute-start.2 = (f32[512,128]{1,0:T(8,128)S(1)}, f32[512,128]{1,0:T(8,128)S(1)}, u32[]{:S(2)}, u32[]{:S(2)}) collective-permute-start(f32[512,128]{1,0:T(8,128)S(1)} %get-tuple-element.28), channel_id=1, source_target_pairs={{0,6},{1,7},{8,14},{9,15},{16,22},{17,23},{24,30},{25,31},{32,38},... | collective-permute-start | bytes 786440 | tf_op jit(solution)/shard_map/ppermute | solution.py:25
  6.4 6.8 %collective-permute-start = (f32[512,128]{1,0:T(8,128)S(1)}, f32[512,128]{1,0:T(8,128)S(1)}, u32[]{:S(2)}, u32[]{:S(2)}) collective-permute-start(f32[512,128]{1,0:T(8,128)S(1)} %get-tuple-element.29), channel_id=1, source_target_pairs={{0,2},{1,3},{8,10},{9,11},{16,18},{17,19},{24,26},{25,27},{32,34},... | collective-permute-start | bytes 786440 | tf_op jit(solution)/shard_map/ppermute | solution.py:24
  14.3 9.0 %collective-permute-start.3 = (f32[512,128]{1,0:T(8,128)S(1)}, f32[512,128]{1,0:T(8,128)S(1)}, u32[]{:S(2)}, u32[]{:S(2)}) collective-permute-start(f32[512,128]{1,0:T(8,128)S(1)} %get-tuple-element.26), channel_id=1, source_target_pairs={{0,6},{6,4},{1,7},{7,5},{8,14},{14,12},{9,15},{15,13},{16,22},{22,... | collective-permute-start | bytes 786440 | tf_op jit(solution)/shard_map/ppermute | solution.py:27
  18.6 6.0 %collective-permute-start.1 = (f32[512,128]{1,0:T(8,128)S(1)}, f32[512,128]{1,0:T(8,128)S(1)}, u32[]{:S(2)}, u32[]{:S(2)}) collective-permute-start(f32[512,128]{1,0:T(8,128)S(1)} %get-tuple-element.27), channel_id=1, source_target_pairs={{0,2},{2,4},{1,3},{3,5},{8,10},{10,12},{9,11},{11,13},{16,18},{18,... | collective-permute-start | bytes 786440 | tf_op jit(solution)/shard_map/ppermute | solution.py:26
  25.8 2.0 %collective-permute-start.4 = (f32[1024,128]{1,0:T(8,128)S(1)}, f32[1024,128]{1,0:T(8,128)S(1)}, u32[]{:S(2)}, u32[]{:S(2)}) collective-permute-start(f32[1024,128]{1,0:T(8,128)S(1)} %pad_maximum_fusion.1), channel_id=1, source_target_pairs={{0,1},{1,0},{2,3},{3,2},{4,5},{5,4},{6,7},{7,6},{8,9},{9,8},{10,11... | collective-permute-start | bytes 1572872 | tf_op jit(solution)/shard_map/ppermute | solution.py:31
  70.5 13.4 %all-to-all-start.3 = ((f32[4,64,256]{2,1,0:T(8,128)}), f32[4,64,256]{2,1,0:T(8,128)S(1)}, u32[]{:S(2)}, u32[]{:S(2)}) async-start(f32[4,64,256]{2,1,0:T(8,128)} %broadcast_in_dim.30), calls=%async_computation.3 | async-start | bytes 524288 | tf_op jit(solution)/shard_map/all_to_all | solution.py:124
  84.0 17.2 %all-to-all-start.4 = ((f32[4,64,1280]{2,1,0:T(8,128)}), f32[4,64,1280]{2,1,0:T(8,128)S(1)}, u32[]{:S(2)}, u32[]{:S(2)}) async-start(f32[4,64,1280]{2,1,0:T(8,128)} %bitcast.61), calls=%async_computation.4 | async-start | bytes 2621440 | tf_op jit(solution)/shard_map/all_to_all | solution.py:117
  102.0 75.4 %copy-start = (f32[1024,256]{1,0:T(8,128)S(1)}, f32[1024,256]{1,0:T(8,128)}, u32[]{:S(2)}) copy-start(f32[1024,256]{1,0:T(8,128)} %pad_maximum_fusion.p_ref) | copy-start | bytes 3145732
  102.0 25.8 %all-to-all-start.5 = ((f32[8,8,1280]{2,1,0:T(8,128)}), f32[8,8,1280]{2,1,0:T(8,128)S(1)}, u32[]{:S(2)}, u32[]{:S(2)}) async-start(f32[8,8,1280]{2,1,0:T(8,128)} %bitcast.13), calls=%async_computation.5 | async-start | bytes 655360 | tf_op jit(solution)/shard_map/all_to_all | solution.py:117
  128.6 18.1 %all-to-all-start.6 = ((f32[8,8,1280]{2,1,0:T(8,128)}), f32[8,8,1280]{2,1,0:T(8,128)S(1)}, u32[]{:S(2)}, u32[]{:S(2)}) async-start(f32[8,8,1280]{2,1,0:T(8,128)} %broadcast_in_dim.31), calls=%async_computation.6 | async-start | bytes 655360 | tf_op jit(solution)/shard_map/all_to_all | solution.py:124
  147.9 29.5 %all-to-all-start.7 = ((f32[4,64,1280]{2,1,0:T(8,128)}), f32[4,64,1280]{2,1,0:T(8,128)S(1)}, u32[]{:S(2)}, u32[]{:S(2)}) async-start(f32[4,64,1280]{2,1,0:T(8,128)} %broadcast_in_dim.33), calls=%async_computation.7 | async-start | bytes 2621440 | tf_op jit(solution)/shard_map/all_to_all | solution.py:124

commit v2 on v1

v2 whole, which is shorter than its diff:
```python
import jax
import jax.numpy as jnp
from jax import lax
from jax.experimental import pallas as pl
from jax.experimental.pallas import tpu as pltpu
from jax.sharding import Mesh, PartitionSpec as P

PRECISE = lax.Precision.HIGHEST
NZ, NY, NX, NC = 8, 4, 4, 2
LANES, SUB = 128, 8
NT = (((1,), (1,)), ((), ()))
VMEM_BYTES = 48 << 20


def dot(left, right, dims=(((1,), (0,)), ((), ()))):
    return lax.dot_general(left, right, dims, precision=PRECISE, preferred_element_type=jnp.float32)


def pick(index, choices):
    value = choices[-1]
    for at in range(len(choices) - 2, -1, -1):
        value = jnp.where(index == at, choices[at], value)
    return value


def relay(own):
    x = lax.axis_index("x")
    half = own.shape[0] // 2
    low, high = own[:half], own[half:]
    up_low = lax.ppermute(low, "x", [(0, 1)])
    down_high = lax.ppermute(high, "x", [(0, 3)])
    up_high = lax.ppermute(high, "x", [(0, 1)])
    down_low = lax.ppermute(low, "x", [(0, 3)])
    on_low = lax.ppermute(up_low, "x", [(1, 2)])
    on_high = lax.ppermute(down_high, "x", [(3, 2)])
    mine_low = pick(x, [low, up_low, on_low, down_low])
    mine_high = pick(x, [high, up_high, on_high, down_high])
    swap = [(0, 1), (1, 0)]
    return mine_low, mine_high, lax.ppermute(mine_low, "c", swap), lax.ppermute(mine_high, "c", swap)


def products_kernel(core_ref, ml_ref, mh_ref, ol_ref, oh_ref, c_ref, o_ref, p_ref, pt_ref):
    i = pl.program_id(0)
    half, k = ml_ref.shape

    @pl.when(i == 0)
    def _():
        first = core_ref[0] == 0
        for rows, m_ref, t_ref in ((slice(0, half), ml_ref, ol_ref), (slice(half, 2 * half), mh_ref, oh_ref)):
            mine, other = m_ref[...], t_ref[...]
            p_ref[rows, :k] = jnp.where(first, mine, other)
            p_ref[rows, k:] = jnp.where(first, other, mine)
        pt_ref[...] = p_ref[...].T
        o_ref[...] = dot(pt_ref[...], p_ref[...])

    @pl.when(i > 0)
    def _():
        o_ref[...] = dot(pt_ref[...], jnp.concatenate([c_ref[0], c_ref[1]], axis=1))


def products(pieces, columns):
    rounds, n, k = columns.shape
    w = 2 * k
    core = lax.axis_index("c").astype(jnp.int32)[None]
    whole = pl.BlockSpec((n // 2, k), lambda i: (0, 0))
    return pl.pallas_call(
        products_kernel,
        grid=(rounds // 2 + 1,),
        in_specs=[pl.BlockSpec(memory_space=pltpu.SMEM)]
        + [whole] * 4
        + [pl.BlockSpec((2, n, k), lambda i: (jnp.maximum(i - 1, 0), 0, 0))],
        out_specs=[pl.BlockSpec((w, w), lambda i: (0, i)), pl.BlockSpec((n, w), lambda i: (0, 0))],
        out_shape=[
            jax.ShapeDtypeStruct((w, w + rounds * k), jnp.float32),
            jax.ShapeDtypeStruct((n, w), jnp.float32),
        ],
        scratch_shapes=[pltpu.VMEM((w, n), jnp.float32)],
        compiler_params=pltpu.CompilerParams(vmem_limit_bytes=VMEM_BYTES),
        name="products",
    )(core, *pieces, columns)


def inverse_root(d):
    y = lax.rsqrt(d)
    return y * (1.5 - 0.5 * d * y * y)


def invert_factor(block, w_ref, row0, col0):
    n = LANES
    tiles = n // SUB
    a = [block[SUB * t:SUB * (t + 1)] for t in range(tiles)]
    lane = lax.broadcasted_iota(jnp.int32, (SUB, LANES), 1)
    sub = lax.broadcasted_iota(jnp.int32, (SUB, LANES), 0)
    b = [jnp.where(lane == sub + SUB * t, 1.0, 0.0).astype(jnp.float32) for t in range(tiles)]

    def across(v, j):
        return jnp.broadcast_to(v[:, j:j + 1], (SUB, LANES))

    def down(v, s):
        return jnp.broadcast_to(v[s:s + 1, :], (SUB, LANES))

    for q in range(n // 4):
        t, s, j = q // 2, (q % 2) * 4, 4 * q
        ra = [down(a[t], s + k) for k in range(4)]
        rb = [down(b[t], s + k) for k in range(4)]
        d = {}
        for x in range(4):
            for y in range(x + 1):
                d[x, y] = across(ra[y], j + x)
                d[y, x] = d[x, y]
        det = 1.0 / (d[0, 0] * d[1, 1] - d[1, 0] * d[1, 0])
        p00, p01, p11 = d[1, 1] * det, -d[1, 0] * det, d[0, 0] * det
        z = [[d[r, 0] * p00 + d[r, 1] * p01, d[r, 0] * p01 + d[r, 1] * p11] for r in (2, 3)]
        s00 = d[2, 2] - (z[0][0] * d[2, 0] + z[0][1] * d[2, 1])
        s01 = d[3, 2] - (z[1][0] * d[2, 0] + z[1][1] * d[2, 1])
        s11 = d[3, 3] - (z[1][0] * d[3, 0] + z[1][1] * d[3, 1])
        sdet = 1.0 / (s00 * s11 - s01 * s01)
        i00, i01, i11 = s11 * sdet, -s01 * sdet, s00 * sdet

        def solve(r):
            u0 = p00 * r[0] + p01 * r[1]
            u1 = p01 * r[0] + p11 * r[1]
            v2 = r[2] - (z[0][0] * r[0] + z[0][1] * r[1])
            v3 = r[3] - (z[1][0] * r[0] + z[1][1] * r[1])
            y2 = i00 * v2 + i01 * v3
            y3 = i01 * v2 + i11 * v3
            return [u0 - (z[0][0] * y2 + z[1][0] * y3), u1 - (z[0][1] * y2 + z[1][1] * y3), y2, y3]

        ya, yb = solve(ra), solve(rb)
        for u in range(t, tiles):
            if u == t and s == 4:
                continue
            c = [across(a[u], j + k) for k in range(4)]
            na, nb = a[u], b[u]
            fa = (c[0] * ya[0] + c[1] * ya[1]) + (c[2] * ya[2] + c[3] * ya[3])
            fb = (c[0] * yb[0] + c[1] * yb[1]) + (c[2] * yb[2] + c[3] * yb[3])
            if u == t:
                a[u] = jnp.where(sub >= 4, na - fa, na)
                b[u] = jnp.where(sub >= 4, nb - fb, nb)
            else:
                a[u], b[u] = na - fa, nb - fb
        k0 = inverse_root(d[0, 0])
        l10 = d[1, 0] * k0
        k1 = inverse_root(d[1, 1] - l10 * l10)
        w0 = k0 * rb[0]
        w1 = k1 * (rb[1] - l10 * w0)
        k2 = inverse_root(s00)
        l32 = s01 * k2
        k3 = inverse_root(s11 - l32 * l32)
        v2 = rb[2] - (z[0][0] * rb[0] + z[0][1] * rb[1])
        v3 = rb[3] - (z[1][0] * rb[0] + z[1][1] * rb[1])
        w2 = k2 * v2
        w3 = k3 * (v3 - l32 * w2)
        for k, w in enumerate((w0, w1, w2, w3)):
            w_ref[row0 + j + k:row0 + j + k + 1, col0:col0 + LANES] = w[0:1]


def factor_kernel(y_ref, g0_ref, g1_ref, g2_ref, g3_ref, p_ref, w_ref, q_ref, g_ref):
    part, h = g0_ref.shape[0], LANES
    y = y_ref[0]
    for step, block in enumerate((g0_ref, g1_ref, g2_ref, g3_ref)):
        at = pl.multiple_of(((y + step) % NY) * part, part)
        g_ref[pl.ds(at, part), :] = block[...]
    invert_factor(g_ref[:h, :h], w_ref, 0, 0)
    w_ref[:h, h:] = jnp.zeros((h, h), jnp.float32)
    w11 = w_ref[:h, :h]
    l21 = dot(g_ref[h:, :h], w11, NT)
    invert_factor(g_ref[h:, h:] - dot(l21, l21, NT), w_ref, h, h)
    w_ref[h:, :h] = -dot(w_ref[h:, h:], dot(l21, w11))
    q_ref[...] = dot(p_ref[...], w_ref[...], NT)


def factor(parts, panels):
    n, w = panels.shape
    y = lax.axis_index("y").astype(jnp.int32)[None]
    vmem = pl.BlockSpec(memory_space=pltpu.VMEM)
    return pl.pallas_call(
        factor_kernel,
        in_specs=[pl.BlockSpec(memory_space=pltpu.SMEM)] + [vmem] * 5,
        out_shape=[jax.ShapeDtypeStruct((w, w), jnp.float32), jax.ShapeDtypeStruct((n, w), jnp.float32)],
        scratch_shapes=[pltpu.VMEM((w, w), jnp.float32)],
        compiler_params=pltpu.CompilerParams(vmem_limit_bytes=VMEM_BYTES),
        name="factor",
    )(y, *parts, panels)


def update_kernel(w_ref, x_ref, q_ref, c_ref, red_ref, top_ref):
    k = c_ref.shape[2]
    top = dot(w_ref[...], x_ref[...])
    fit = dot(q_ref[...], top)
    for at in range(2):
        top_ref[at] = top[:, at * k : (at + 1) * k]
        red_ref[at] = c_ref[at] - fit[:, at * k : (at + 1) * k]


def update(inverse, basis, cross, columns):
    rounds, n, k = columns.shape
    w = inverse.shape[0]
    return pl.pallas_call(
        update_kernel,
        grid=(rounds // 2,),
        in_specs=[
            pl.BlockSpec((w, w), lambda i: (0, 0)),
            pl.BlockSpec((w, 2 * k), lambda i: (0, i)),
            pl.BlockSpec((n, w), lambda i: (0, 0)),
            pl.BlockSpec((2, n, k), lambda i: (i, 0, 0)),
        ],
        out_specs=[
            pl.BlockSpec((2, n, k), lambda i: (i, 0, 0)),
            pl.BlockSpec((2, w, k), lambda i: (i, 0, 0)),
        ],
        out_shape=[
            jax.ShapeDtypeStruct((rounds, n, k), jnp.float32),
            jax.ShapeDtypeStruct((rounds, w, k), jnp.float32),
        ],
        compiler_params=pltpu.CompilerParams(vmem_limit_bytes=VMEM_BYTES),
        name="update",
    )(inverse, cross, basis, columns)


def scatter_sum(values, axis, parts):
    rows, width = values.shape
    pieces = lax.all_to_all(values.reshape(parts, rows // parts, width), axis, 0, 0)
    return jnp.sum(pieces, axis=0)


def gather(values, axis, parts):
    rows, width = values.shape
    copies = jnp.broadcast_to(values[None], (parts, rows, width))
    return lax.all_to_all(copies, axis, 0, 0).reshape(parts * rows, width)


def shards(matrix):
    columns = jnp.transpose(matrix, (1, 0, 2))
    both, panels = products(relay(columns[0]), columns)
    part = scatter_sum(both, "y", NY)
    part = scatter_sum(part, "z", NZ)
    part = gather(part, "z", NZ)
    w = panels.shape[1]
    gram_part, cross_part = part[:, :w], part[:, w:]
    ahead = [lax.ppermute(gram_part, "y", [(y, (y - by) % NY) for y in range(NY)]) for by in (1, 2, 3)]
    inverse, basis = factor([gram_part, *ahead], panels)
    cross = gather(cross_part, "y", NY)
    reduced, top = update(inverse, basis, cross, columns)
    return jnp.transpose(reduced, (1, 0, 2)), jnp.transpose(top, (1, 0, 2))


def solution(mesh):
    fine = Mesh(mesh.devices.reshape(NZ, NY, NX, NC), ("z", "y", "x", "c"))
    return jax.shard_map(
        shards,
        mesh=fine,
        in_specs=(P(("z", "y"), None, ("x", "c")),),
        out_specs=(P(("z", "y"), None, ("x", "c")), P(None, None, ("x", "c"))),
        check_vma=False,
    )
```

time: 192 us -> 150 us (0.78)
  the two profiles are of different devices: /device:TPU:8 before, /device:TPU:4 now
where the time goes in v2:
time: 150 us; the launch traced here: 149 us
  blocking collectives  62.6 us (42%)
  Pallas kernels  33 us (22%)
  waiting for transfers between devices  27.3 us (18%)
  starting transfers between devices  15.5 us (10%)
  local copies, waits for them, and re-layouts  6.87 us (5%)
  other arithmetic  2.68 us (2%)
    all_to_all x2, blocking collectives, scatter_sum(): lax.all_to_all(values.reshape(parts, rows // parts, width), axis, 0, 0)  47.2 us
    all_to_all x1, blocking collectives, gather(): return lax.all_to_all(copies, axis, 0, 0).reshape(parts * rows, width)  15.5 us
    ppermute x1, waiting for transfers between devices, relay(): on_high = lax.ppermute(down_high, 'x', [(3, 2)])  13.7 us
    pallas_call x1, Pallas kernels, factor(): pl.pallas_call(factor_kernel, in_specs=[pl.BlockSpec(memory_space=pltpu.S...  13.6 us
    ppermute x3, waiting for transfers between devices, shards(): lax.ppermute(gram_part, 'y', [(y, (y - by) % NY) for y in range(NY)])  11.4 us
    pallas_call x1, Pallas kernels, update(): pl.pallas_call(update_kernel, grid=(rounds // 2,), in_specs=[pl.BlockSpec...  11 us
    pallas_call x1, Pallas kernels, products(): pl.pallas_call(products_kernel, grid=(rounds // 2 + 1,), in_specs=[pl.Blo...  8.46 us
    ppermute x3, starting transfers between devices, shards(): lax.ppermute(gram_part, 'y', [(y, (y - by) % NY) for y in range(NY)])  6.12 us
  transfers between devices with their start and end apart: 12, of which 6 were waited for; matrix products, arithmetic and copies ran while one was open for 0% of the time, Pallas kernels for 9%

profile of v2, /device:TPU:4, one launch (start us, length us, event | category | flops | bytes accessed | tf_op | source)
XLA Modules:
  0.0 148.8 jit_solution(1400963551293500134)
XLA Ops:
  0.6 1.1 slice_bitcast_fusion
  1.7 0.7 collective-permute-start.4
  2.4 0.7 collective-permute-start
  3.1 0.7 collective-permute-start.3
  3.8 0.7 collective-permute-start.2
  4.4 0.0 collective-permute-done.4
  4.5 1.3 collective-permute-start.5
  5.8 0.0 collective-permute-done
  5.8 1.3 collective-permute-start.1
  7.1 0.0 collective-permute-done.3
  7.1 0.0 collective-permute-done.2
  7.1 13.7 %collective-permute-done.5 = f32[512,128]{1,0:T(8,128)S(1)} collective-permute-done((f32[512,128]{1,0:T(8,128)S(1)}, f32[512,128]{1,0:T(8,128)S(1)}, u32[]{:S(2)}, u32[]{:S(2)}) %collective-permute-start.5) | collective-permute-done | bytes 262176 | tf_op jit(solution)/shard_map/ppermute | solution.py:35
  20.8 0.7 collective-permute-done.1
  21.5 1.1 select_select_fusion
  22.6 0.1 collective-permute-start.7
  22.7 0.5 collective-permute-start.6
  23.2 1.0 collective-permute-done.7.oh_ref
  24.3 0.4 collective-permute-done.6.ol_ref
  24.6 8.5 %products.1 = (f32[256,1536]{1,0:T(8,128)S(1)}, f32[1024,256]{1,0:T(8,128)S(1)}) custom-call(s32[1]{0:T(128)} %bitcast.1.core_ref, f32[512,128]{1,0:T(8,128)S(1)} %get-tuple-element.15.ml_ref, f32[512,128]{1,0:T(8,128)S(1)} %get-tuple-element.14.mh_ref, f32[512,128]{1,0:T(8,128)S(1)} %collective-permute-done.6.ol_ref, ...), custom_call_target="tpu_custom_call" | custom-call | tf_op jit(solution)/shard_map/products/pallas_call | solution.py:66
  33.1 25.4 %all_to_all.20 = f32[4,64,1536]{2,1,0:T(8,128)} all-to-all(f32[4,64,1536]{2,1,0:T(8,128)S(1)} %bitcast.18), channel_id=1, replica_groups=mesh['z'=8,'y'=4,'x'=4,'c'=2] {'y'}, dimensions={0} | all-to-all | bytes 3145728 | tf_op jit(solution)/shard_map/all_to_all | solution.py:223
  58.5 1.5 %reduce_sum.18 = f32[64,1536]{1,0:T(8,128)S(1)} reduce(f32[4,64,1536]{2,1,0:T(8,128)} %all_to_all.20, f32[]{:T(128)} %constant.18.clone.1), dimensions={0}, to_apply=%region_0.1 | reduce | flops 294912 | bytes 1966084 | tf_op jit(solution)/shard_map/reduce_sum | solution.py:224
  60.0 21.8 %all_to_all.21 = f32[8,8,1536]{2,1,0:T(8,128)S(1)} all-to-all(f32[8,8,1536]{2,1,0:T(8,128)S(1)} %bitcast.25), channel_id=1, replica_groups=mesh['z'=8,'y'=4,'x'=4,'c'=2] {'z'}, dimensions={0} | all-to-all | bytes 786432 | tf_op jit(solution)/shard_map/all_to_all | solution.py:223
  81.9 15.5 %all_to_all.22 = f32[8,8,1536]{2,1,0:T(8,128)S(1)} all-to-all(f32[8,8,1536]{2,1,0:T(8,128)S(1)} %broadcast_in_dim.20), channel_id=1, replica_groups=mesh['z'=8,'y'=4,'x'=4,'c'=2] {'z'}, dimensions={0} | all-to-all | bytes 786432 | tf_op jit(solution)/shard_map/all_to_all | solution.py:230
  97.4 1.2 broadcast_in_dim.21
  98.5 3.5 %all-to-all-start.3 = ((f32[4,64,1280]{2,1,0:T(8,128)}), f32[4,64,1280]{2,1,0:T(8,128)S(1)}, u32[]{:S(2)}, u32[]{:S(2)}) async-start(f32[4,64,1280]{2,1,0:T(8,128)} %broadcast_in_dim.21), calls=%async_computation.3 | async-start | bytes 2621440 | tf_op jit(solution)/shard_map/all_to_all | solution.py:230
  102.1 2.0 %collective-permute-start.10 = (f32[64,256]{1,0:T(8,128)S(1)}, f32[64,256]{1,0:T(8,128)S(1)}, u32[]{:S(2)}, u32[]{:S(2)}) collective-permute-start(f32[64,256]{1,0:T(8,128)S(1)} %slice.29.g0_ref), channel_id=1, source_target_pairs={{0,8},{8,16},{16,24},{24,0},{1,9},{9,17},{17,25},{25,1},{2,10},{10... | collective-permute-start | bytes 196616 | tf_op jit(solution)/shard_map/ppermute | solution.py:241
  104.1 2.7 %collective-permute-start.9 = (f32[64,256]{1,0:T(8,128)S(1)}, f32[64,256]{1,0:T(8,128)S(1)}, u32[]{:S(2)}, u32[]{:S(2)}) collective-permute-start(f32[64,256]{1,0:T(8,128)S(1)} %slice.29.g0_ref), channel_id=1, source_target_pairs={{0,16},{8,24},{16,0},{24,8},{1,17},{9,25},{17,1},{25,9},{2,18},{10... | collective-permute-start | bytes 196616 | tf_op jit(solution)/shard_map/ppermute | solution.py:241
  106.8 1.5 collective-permute-start.8
  108.2 10.3 %collective-permute-done.10.g3_ref = f32[64,256]{1,0:T(8,128)S(1)} collective-permute-done((f32[64,256]{1,0:T(8,128)S(1)}, f32[64,256]{1,0:T(8,128)S(1)}, u32[]{:S(2)}, u32[]{:S(2)}) %collective-permute-start.10) | collective-permute-done | bytes 65568 | tf_op jit(solution)/shard_map/ppermute | solution.py:241
  118.6 1.1 collective-permute-done.9.g2_ref
  119.6 0.0 copy-start.2
  119.6 0.6 copy-done.2
  120.3 0.0 collective-permute-done.8.g1_ref
  120.3 0.0 copy-start.4
  120.3 0.6 copy-done.4
  120.9 0.0 copy-start.3
  120.9 0.8 copy-done.3
  121.8 0.0 copy-start.5
  121.8 0.8 copy-done.5
  122.6 13.6 %factor.1 = (f32[256,256]{1,0:T(8,128)S(1)}, f32[1024,256]{1,0:T(8,128)S(1)}) custom-call(s32[1]{0:T(128)} %bitcast.y_ref, f32[64,256]{1,0:T(8,128)S(1)} %slice.29.g0_ref, f32[64,256]{1,0:T(8,128)S(1)} %copy-done.5, f32[64,256]{1,0:T(8,128)S(1)} %copy-done.3, f32[64,256]{1,0:T(8,128)S(1)} %collective-permute-done.10.g3_ref, ...), custom_call_target="tpu_custom_call" | custom-call | tf_op jit(solution)/shard_map/factor/pallas_call | solution.py:177
  136.2 0.0 copy-start
  136.2 0.7 copy-done
  136.9 0.0 all-to-all-done.3
  136.9 0.0 copy-start.1
  136.9 0.9 copy-done.1
  137.9 11.0 %update.1 = (f32[10,1024,128]{2,1,0:T(8,128)}, f32[10,256,128]{2,1,0:T(8,128)}) custom-call(f32[256,256]{1,0:T(8,128)S(1)} %copy-done.1, f32[256,1280]{1,0:T(8,128)S(1)} %bitcast.17, f32[1024,256]{1,0:T(8,128)S(1)} %get-tuple-element.11.q_ref, f32[10,1024,128]{2,1,0:T(8,128)} %bitcast.22), custom_call_target="tpu_custom_call" | custom-call | tf_op jit(solution)/shard_map/update/pallas_call | solution.py:199
  (4 shorter events, 0.1 us)
Async XLA Ops:
  1.7 2.7 %collective-permute-start.4 = (f32[512,128]{1,0:T(8,128)S(1)}, f32[512,128]{1,0:T(8,128)S(1)}, u32[]{:S(2)}, u32[]{:S(2)}) collective-permute-start(f32[512,128]{1,0:T(8,128)S(1)} %get-tuple-element.16), channel_id=1, source_target_pairs={{0,6},{1,7},{8,14},{9,15},{16,22},{17,23},{24,30},{25,31},{32,38},... | collective-permute-start | bytes 786440 | tf_op jit(solution)/shard_map/ppermute | solution.py:31
  2.4 3.4 %collective-permute-start = (f32[512,128]{1,0:T(8,128)S(1)}, f32[512,128]{1,0:T(8,128)S(1)}, u32[]{:S(2)}, u32[]{:S(2)}) collective-permute-start(f32[512,128]{1,0:T(8,128)S(1)} %get-tuple-element.17), channel_id=1, source_target_pairs={{0,2},{1,3},{8,10},{9,11},{16,18},{17,19},{24,26},{25,27},{32,34},... | collective-permute-start | bytes 786440 | tf_op jit(solution)/shard_map/ppermute | solution.py:30
  3.1 4.0 %collective-permute-start.3 = (f32[512,128]{1,0:T(8,128)S(1)}, f32[512,128]{1,0:T(8,128)S(1)}, u32[]{:S(2)}, u32[]{:S(2)}) collective-permute-start(f32[512,128]{1,0:T(8,128)S(1)} %get-tuple-element.16), channel_id=1, source_target_pairs={{0,2},{1,3},{8,10},{9,11},{16,18},{17,19},{24,26},{25,27},{32,34},... | collective-permute-start | bytes 786440 | tf_op jit(solution)/shard_map/ppermute | solution.py:32
  3.8 3.3 %collective-permute-start.2 = (f32[512,128]{1,0:T(8,128)S(1)}, f32[512,128]{1,0:T(8,128)S(1)}, u32[]{:S(2)}, u32[]{:S(2)}) collective-permute-start(f32[512,128]{1,0:T(8,128)S(1)} %get-tuple-element.17), channel_id=1, source_target_pairs={{0,6},{1,7},{8,14},{9,15},{16,22},{17,23},{24,30},{25,31},{32,38},... | collective-permute-start | bytes 786440 | tf_op jit(solution)/shard_map/ppermute | solution.py:33
  4.5 16.4 %collective-permute-start.5 = (f32[512,128]{1,0:T(8,128)S(1)}, f32[512,128]{1,0:T(8,128)S(1)}, u32[]{:S(2)}, u32[]{:S(2)}) collective-permute-start(f32[512,128]{1,0:T(8,128)S(1)} %collective-permute-done.4), channel_id=1, source_target_pairs={{6,4},{7,5},{14,12},{15,13},{22,20},{23,21},{30,28},{31,29},{38,36... | collective-permute-start | bytes 786440 | tf_op jit(solution)/shard_map/ppermute | solution.py:35
  5.8 15.8 %collective-permute-start.1 = (f32[512,128]{1,0:T(8,128)S(1)}, f32[512,128]{1,0:T(8,128)S(1)}, u32[]{:S(2)}, u32[]{:S(2)}) collective-permute-start(f32[512,128]{1,0:T(8,128)S(1)} %collective-permute-done), channel_id=1, source_target_pairs={{2,4},{3,5},{10,12},{11,13},{18,20},{19,21},{26,28},{27,29},{34,36... | collective-permute-start | bytes 786440 | tf_op jit(solution)/shard_map/ppermute | solution.py:34
  22.6 1.6 %collective-permute-start.7 = (f32[512,128]{1,0:T(8,128)S(1)}, f32[512,128]{1,0:T(8,128)S(1)}, u32[]{:S(2)}, u32[]{:S(2)}) collective-permute-start(f32[512,128]{1,0:T(8,128)S(1)} %get-tuple-element.14.mh_ref), channel_id=1, source_target_pairs={{0,1},{1,0},{2,3},{3,2},{4,5},{5,4},{6,7},{7,6},{8,9},{9,8},{10,11... | collective-permute-start | bytes 786440 | tf_op jit(solution)/shard_map/ppermute | solution.py:39
  22.7 1.9 %collective-permute-start.6 = (f32[512,128]{1,0:T(8,128)S(1)}, f32[512,128]{1,0:T(8,128)S(1)}, u32[]{:S(2)}, u32[]{:S(2)}) collective-permute-start(f32[512,128]{1,0:T(8,128)S(1)} %get-tuple-element.15.ml_ref), channel_id=1, source_target_pairs={{0,1},{1,0},{2,3},{3,2},{4,5},{5,4},{6,7},{7,6},{8,9},{9,8},{10,11... | collective-permute-start | bytes 786440 | tf_op jit(solution)/shard_map/ppermute | solution.py:39
  98.5 38.4 %all-to-all-start.3 = ((f32[4,64,1280]{2,1,0:T(8,128)}), f32[4,64,1280]{2,1,0:T(8,128)S(1)}, u32[]{:S(2)}, u32[]{:S(2)}) async-start(f32[4,64,1280]{2,1,0:T(8,128)} %broadcast_in_dim.21), calls=%async_computation.3 | async-start | bytes 2621440 | tf_op jit(solution)/shard_map/all_to_all | solution.py:230
  102.1 16.5 %collective-permute-start.10 = (f32[64,256]{1,0:T(8,128)S(1)}, f32[64,256]{1,0:T(8,128)S(1)}, u32[]{:S(2)}, u32[]{:S(2)}) collective-permute-start(f32[64,256]{1,0:T(8,128)S(1)} %slice.29.g0_ref), channel_id=1, source_target_pairs={{0,8},{8,16},{16,24},{24,0},{1,9},{9,17},{17,25},{25,1},{2,10},{10... | collective-permute-start | bytes 196616 | tf_op jit(solution)/shard_map/ppermute | solution.py:241
  104.1 15.6 %collective-permute-start.9 = (f32[64,256]{1,0:T(8,128)S(1)}, f32[64,256]{1,0:T(8,128)S(1)}, u32[]{:S(2)}, u32[]{:S(2)}) collective-permute-start(f32[64,256]{1,0:T(8,128)S(1)} %slice.29.g0_ref), channel_id=1, source_target_pairs={{0,16},{8,24},{16,0},{24,8},{1,17},{9,25},{17,1},{25,9},{2,18},{10... | collective-permute-start | bytes 196616 | tf_op jit(solution)/shard_map/ppermute | solution.py:241
  106.8 13.5 %collective-permute-start.8 = (f32[64,256]{1,0:T(8,128)S(1)}, f32[64,256]{1,0:T(8,128)S(1)}, u32[]{:S(2)}, u32[]{:S(2)}) collective-permute-start(f32[64,256]{1,0:T(8,128)S(1)} %slice.29.g0_ref), channel_id=1, source_target_pairs={{0,24},{8,0},{16,8},{24,16},{1,25},{9,1},{17,9},{25,17},{2,26},{10... | collective-permute-start | bytes 196616 | tf_op jit(solution)/shard_map/ppermute | solution.py:241
  119.6 0.6 copy-start.2
  120.3 0.6 copy-start.4
  120.9 0.8 copy-start.3
  121.8 0.8 copy-start.5
  136.2 0.7 copy-start
  136.9 1.0 copy-start.1

commit v3 on v2

--- a/solution.py
+++ b/solution.py
@@ -9,7 +9,7 @@
 NZ, NY, NX, NC = 8, 4, 4, 2
 LANES, SUB = 128, 8
 NT = (((1,), (1,)), ((), ()))
-VMEM_BYTES = 48 << 20
+PARAMS = pltpu.CompilerParams(vmem_limit_bytes=48 << 20)
 
 
 def dot(left, right, dims=(((1,), (0,)), ((), ()))):
@@ -23,61 +23,79 @@
     return value
 
 
-def relay(own):
-    x = lax.axis_index("x")
-    half = own.shape[0] // 2
-    low, high = own[:half], own[half:]
-    up_low = lax.ppermute(low, "x", [(0, 1)])
-    down_high = lax.ppermute(high, "x", [(0, 3)])
-    up_high = lax.ppermute(high, "x", [(0, 1)])
-    down_low = lax.ppermute(low, "x", [(0, 3)])
-    on_low = lax.ppermute(up_low, "x", [(1, 2)])
-    on_high = lax.ppermute(down_high, "x", [(3, 2)])
-    mine_low = pick(x, [low, up_low, on_low, down_low])
-    mine_high = pick(x, [high, up_high, on_high, down_high])
-    swap = [(0, 1), (1, 0)]
-    return mine_low, mine_high, lax.ppermute(mine_low, "c", swap), lax.ppermute(mine_high, "c", swap)
-
-
-def products_kernel(core_ref, ml_ref, mh_ref, ol_ref, oh_ref, c_ref, o_ref, p_ref, pt_ref):
-    i = pl.program_id(0)
-    half, k = ml_ref.shape
-
-    @pl.when(i == 0)
+def spread_x(values):
+    return [values] + [lax.ppermute(values, "x", [(0, to)]) for to in (1, 2, 3)]
+
+
+def swap(values):
+    return lax.ppermute(values, "c", [(0, 1), (1, 0)])
+
+
+def index_of(axis):
+    return lax.axis_index(axis).astype(jnp.int32)[None]
+
+
+SCALAR = pl.BlockSpec(memory_space=pltpu.SMEM)
+
+
+def whole(shape):
+    return pl.BlockSpec(shape, lambda i: (0,) * len(shape))
+
+
+def place(core_ref, mine_ref, other_ref, p_ref):
+    k = mine_ref.shape[1]
+    first = core_ref[0] == 0
+    mine, other = mine_ref[...], other_ref[...]
+    p_ref[:, :k] = jnp.where(first, mine, other)
+    p_ref[:, k:] = jnp.where(first, other, mine)
+
+
+def gram_kernel(core_ref, mine_ref, other_ref, g_ref, p_ref):
+    place(core_ref, mine_ref, other_ref, p_ref)
+    panels = p_ref[...]
+    g_ref[...] = dot(panels.T, panels)
+
+
+def gram_of(mine, other):
+    n, k = mine.shape
+    w = 2 * k
+    return pl.pallas_call(
+        gram_kernel,
+        grid=(1,),
+        in_specs=[SCALAR, whole((n, k)), whole((n, k))],
+        out_specs=whole((w, w)),
+        out_shape=jax.ShapeDtypeStruct((w, w), jnp.float32),
+        scratch_shapes=[pltpu.VMEM((n, w), jnp.float32)],
+        compiler_params=PARAMS,
+        name="gram",
+    )(index_of("c"), mine, other)
+
+
+def cross_kernel(core_ref, mine_ref, other_ref, c_ref, o_ref, p_ref, pt_ref):
+    @pl.when(pl.program_id(0) == 0)
     def _():
-        first = core_ref[0] == 0
-        for rows, m_ref, t_ref in ((slice(0, half), ml_ref, ol_ref), (slice(half, 2 * half), mh_ref, oh_ref)):
-            mine, other = m_ref[...], t_ref[...]
-            p_ref[rows, :k] = jnp.where(first, mine, other)
-            p_ref[rows, k:] = jnp.where(first, other, mine)
+        place(core_ref, mine_ref, other_ref, p_ref)
         pt_ref[...] = p_ref[...].T
-        o_ref[...] = dot(pt_ref[...], p_ref[...])
-
-    @pl.when(i > 0)
-    def _():
-        o_ref[...] = dot(pt_ref[...], jnp.concatenate([c_ref[0], c_ref[1]], axis=1))
-
-
-def products(pieces, columns):
+
+    o_ref[...] = dot(pt_ref[...], jnp.concatenate([c_ref[0], c_ref[1]], axis=1))
+
+
+def cross_of(mine, other, columns):
     rounds, n, k = columns.shape
     w = 2 * k
-    core = lax.axis_index("c").astype(jnp.int32)[None]
-    whole = pl.BlockSpec((n // 2, k), lambda i: (0, 0))
-    return pl.pallas_call(
-        products_kernel,
-        grid=(rounds // 2 + 1,),
-        in_specs=[pl.BlockSpec(memory_space=pltpu.SMEM)]
-        + [whole] * 4
-        + [pl.BlockSpec((2, n, k), lambda i: (jnp.maximum(i - 1, 0), 0, 0))],
-        out_specs=[pl.BlockSpec((w, w), lambda i: (0, i)), pl.BlockSpec((n, w), lambda i: (0, 0))],
+    return pl.pallas_call(
+        cross_kernel,
+        grid=(rounds // 2,),
+        in_specs=[SCALAR, whole((n, k)), whole((n, k)), pl.BlockSpec((2, n, k), lambda i: (i, 0, 0))],
+        out_specs=[pl.BlockSpec((w, w), lambda i: (0, i)), whole((n, w))],
         out_shape=[
-            jax.ShapeDtypeStruct((w, w + rounds * k), jnp.float32),
+            jax.ShapeDtypeStruct((w, rounds * k), jnp.float32),
             jax.ShapeDtypeStruct((n, w), jnp.float32),
         ],
         scratch_shapes=[pltpu.VMEM((w, n), jnp.float32)],
-        compiler_params=pltpu.CompilerParams(vmem_limit_bytes=VMEM_BYTES),
-        name="products",
-    )(core, *pieces, columns)
+        compiler_params=PARAMS,
+        name="cross",
+    )(index_of("c"), mine, other, columns)
 
 
 def inverse_root(d):
@@ -155,33 +173,58 @@
             w_ref[row0 + j + k:row0 + j + k + 1, col0:col0 + LANES] = w[0:1]
 
 
-def factor_kernel(y_ref, g0_ref, g1_ref, g2_ref, g3_ref, p_ref, w_ref, q_ref, g_ref):
-    part, h = g0_ref.shape[0], LANES
-    y = y_ref[0]
-    for step, block in enumerate((g0_ref, g1_ref, g2_ref, g3_ref)):
-        at = pl.multiple_of(((y + step) % NY) * part, part)
-        g_ref[pl.ds(at, part), :] = block[...]
+def factor_first_kernel(x_ref, *refs):
+    grams, (w_ref, l_ref, s_ref, g_ref) = refs[:NX], refs[NX:]
+    h = LANES
+    for at, gram in enumerate(grams):
+
+        @pl.when(x_ref[0] == at)
+        def _(gram=gram):
+            g_ref[...] = gram[...]
+
     invert_factor(g_ref[:h, :h], w_ref, 0, 0)
+    l21 = dot(g_ref[h:, :h], w_ref[...], NT)
+    l_ref[...] = l21
+    s_ref[...] = g_ref[h:, h:] - dot(l21, l21, NT)
+
+
+def factor_last_kernel(w11_ref, l_ref, s_ref, p_ref, w_ref, q_ref):
+    h = LANES
+    w11 = w11_ref[...]
+    w_ref[:h, :h] = w11
     w_ref[:h, h:] = jnp.zeros((h, h), jnp.float32)
-    w11 = w_ref[:h, :h]
-    l21 = dot(g_ref[h:, :h], w11, NT)
-    invert_factor(g_ref[h:, h:] - dot(l21, l21, NT), w_ref, h, h)
-    w_ref[h:, :h] = -dot(w_ref[h:, h:], dot(l21, w11))
+    invert_factor(s_ref[...], w_ref, h, h)
+    w_ref[h:, :h] = -dot(w_ref[h:, h:], dot(l_ref[...], w11))
     q_ref[...] = dot(p_ref[...], w_ref[...], NT)
 
 
-def factor(parts, panels):
+def factor_first(grams):
+    w = grams[0].shape[0]
+    h = w // 2
+    return pl.pallas_call(
+        factor_first_kernel,
+        grid=(1,),
+        in_specs=[SCALAR] + [whole((w, w))] * NX,
+        out_specs=[whole((h, h))] * 3,
+        out_shape=[jax.ShapeDtypeStruct((h, h), jnp.float32)] * 3,
+        scratch_shapes=[pltpu.VMEM((w, w), jnp.float32)],
+        compiler_params=PARAMS,
+        name="factor_first",
+    )(index_of("x"), *grams)
+
+
+def factor_last(w11, l21, schur, panels):
     n, w = panels.shape
-    y = lax.axis_index("y").astype(jnp.int32)[None]
-    vmem = pl.BlockSpec(memory_space=pltpu.VMEM)
-    return pl.pallas_call(
-        factor_kernel,
-        in_specs=[pl.BlockSpec(memory_space=pltpu.SMEM)] + [vmem] * 5,
+    h = w // 2
+    return pl.pallas_call(
+        factor_last_kernel,
+        grid=(1,),
+        in_specs=[whole((h, h))] * 3 + [whole((n, w))],
+        out_specs=[whole((w, w)), whole((n, w))],
         out_shape=[jax.ShapeDtypeStruct((w, w), jnp.float32), jax.ShapeDtypeStruct((n, w), jnp.float32)],
-        scratch_shapes=[pltpu.VMEM((w, w), jnp.float32)],
-        compiler_params=pltpu.CompilerParams(vmem_limit_bytes=VMEM_BYTES),
-        name="factor",
-    )(y, *parts, panels)
+        compiler_params=PARAMS,
+        name="factor_last",
+    )(w11, l21, schur, panels)
 
 
 def update_kernel(w_ref, x_ref, q_ref, c_ref, red_ref, top_ref):
@@ -213,7 +256,7 @@
             jax.ShapeDtypeStruct((rounds, n, k), jnp.float32),
             jax.ShapeDtypeStruct((rounds, w, k), jnp.float32),
         ],
-        compiler_params=pltpu.CompilerParams(vmem_limit_bytes=VMEM_BYTES),
+        compiler_params=PARAMS,
         name="update",
     )(inverse, cross, basis, columns)
 
@@ -231,16 +274,26 @@
 
 
 def shards(matrix):
+    hold = lax.optimization_barrier
     columns = jnp.transpose(matrix, (1, 0, 2))
-    both, panels = products(relay(columns[0]), columns)
-    part = scatter_sum(both, "y", NY)
+    own = columns[0]
+    arrived = spread_x(own)
+    gram = gram_of(own, swap(own))
+    rows = ("z", "y")
+    gram = scatter_sum(gram, rows, NZ * NY)
+    gram, arrived = hold((gram, arrived))
+    gram = gather(gram, rows, NZ * NY)
+    mine = pick(lax.axis_index("x"), arrived)
+    cross, panels = cross_of(mine, swap(mine), columns)
+    gram, cross = hold((gram, cross))
+    part = scatter_sum(cross, "y", NY)
+    first = factor_first(spread_x(gram))
+    part, first = hold((part, first))
     part = scatter_sum(part, "z", NZ)
+    last = factor_last(*first, panels)
+    part, (inverse, basis) = hold((part, last))
     part = gather(part, "z", NZ)
-    w = panels.shape[1]
-    gram_part, cross_part = part[:, :w], part[:, w:]
-    ahead = [lax.ppermute(gram_part, "y", [(y, (y - by) % NY) for y in range(NY)]) for by in (1, 2, 3)]
-    inverse, basis = factor([gram_part, *ahead], panels)
-    cross = gather(cross_part, "y", NY)
+    cross = gather(part, "y", NY)
     reduced, top = update(inverse, basis, cross, columns)
     return jnp.transpose(reduced, (1, 0, 2)), jnp.transpose(top, (1, 0, 2))
 

time: 150 us -> 143 us (0.953)
  the two profiles are of different devices: /device:TPU:4 before, /device:TPU:2 now
where the time goes in v3:
time: 143 us
  starting transfers between devices  36.4 us (25%)
  Pallas kernels  34.8 us (24%)
  waiting for transfers between devices  34.5 us (24%)
  blocking collectives  31.9 us (22%)
  other arithmetic  2.29 us (2%)
  local copies, waits for them, and re-layouts  1.91 us (1%)
    all_to_all x2, blocking collectives, gather(): return lax.all_to_all(copies, axis, 0, 0).reshape(parts * rows, width)  31.9 us
    all_to_all x3, starting transfers between devices, scatter_sum(): lax.all_to_all(values.reshape(parts, rows // parts, width), axis, 0, 0)  19.4 us
    all_to_all x3, waiting for transfers between devices, scatter_sum(): lax.all_to_all(values.reshape(parts, rows // parts, width), axis, 0, 0)  18.9 us
    all_to_all x1, starting transfers between devices, gather(): return lax.all_to_all(copies, axis, 0, 0).reshape(parts * rows, width)  11.5 us
    pallas_call x1, Pallas kernels, update(): pl.pallas_call(update_kernel, grid=(rounds // 2,), in_specs=[pl.BlockSpec...  11 us
    ppermute x6, waiting for transfers between devices, spread_x(): return [values] + [lax.ppermute(values, 'x', [(0, to)]) for to in (1, 2, 3)]  10.2 us
    pallas_call x1, Pallas kernels, cross_of(): pl.pallas_call(cross_kernel, grid=(rounds // 2,), in_specs=[SCALAR, whole...  8.31 us
    pallas_call x1, Pallas kernels, factor_last(): pl.pallas_call(factor_last_kernel, grid=(1,), in_specs=[whole((h, h))] *...  7.06 us
  transfers between devices with their start and end apart: 12, of which 5 were waited for; matrix products, arithmetic and copies ran while one was open for 1% of the time, Pallas kernels for 17%

profile of v3, /device:TPU:2, one launch (start us, length us, event | category | flops | bytes accessed | tf_op | source)
XLA Modules:
  0.0 142.6 jit_solution(5603906604890909249)
XLA Ops:
  0.6 1.1 slice_bitcast_fusion.mine_ref
  1.7 0.1 collective-permute-start
  1.8 0.7 collective-permute-start.3
  2.5 0.7 collective-permute-start.2
  3.2 1.3 collective-permute-start.1
  4.5 0.0 collective-permute-done.other_ref
  4.5 1.9 %gram.1 = f32[256,256]{1,0:T(8,128)} custom-call(s32[1]{0:T(128)} %bitcast.core_ref, f32[1024,128]{1,0:T(8,128)S(1)} %slice_bitcast_fusion.mine_ref, f32[1024,128]{1,0:T(8,128)S(1)} %collective-permute-done.other_ref), custom_call_target="tpu_custom_call" | custom-call | tf_op jit(solution)/shard_map/gram/pallas_call | solution.py:62
  6.4 11.5 %all-to-all-start = ((f32[32,8,256]{2,1,0:T(8,128)}), f32[32,8,256]{2,1,0:T(8,128)S(1)}, u32[]{:S(2)}, u32[]{:S(2)}) async-start(f32[32,8,256]{2,1,0:T(8,128)} %bitcast.3), calls=%async_computation | async-start | bytes 524288 | tf_op jit(solution)/shard_map/all_to_all | solution.py:266
  18.0 13.7 %all-to-all-done = f32[32,8,256]{2,1,0:T(8,128)S(1)} async-done(((f32[32,8,256]{2,1,0:T(8,128)}), f32[32,8,256]{2,1,0:T(8,128)S(1)}, u32[]{:S(2)}, u32[]{:S(2)}) %all-to-all-start) | async-done | bytes 262176 | tf_op jit(solution)/shard_map/all_to_all | solution.py:266
  31.7 0.0 collective-permute-done.3
  31.7 0.0 collective-permute-done.2
  31.7 0.2 collective-permute-done.1
  31.9 0.1 select_select_fusion.mine_ref
  31.9 0.1 collective-permute-start.4
  32.0 0.7 broadcast_in_dim.13
  32.8 11.5 %all-to-all-start.1 = ((f32[32,8,256]{2,1,0:T(8,128)}), f32[32,8,256]{2,1,0:T(8,128)S(1)}, u32[]{:S(2)}, u32[]{:S(2)}) async-start(f32[32,8,256]{2,1,0:T(8,128)} %broadcast_in_dim.13), calls=%async_computation.1 | async-start | bytes 524288 | tf_op jit(solution)/shard_map/all_to_all | solution.py:273
  44.3 0.0 collective-permute-done.4.other_ref
  44.3 8.3 %cross.1 = (f32[256,1280]{1,0:T(8,128)}, f32[1024,256]{1,0:T(8,128)S(1)}) custom-call(s32[1]{0:T(128)} %bitcast.core_ref, f32[1024,128]{1,0:T(8,128)S(1)} %select_select_fusion.mine_ref, f32[1024,128]{1,0:T(8,128)S(1)} %collective-permute-done.4.other_ref, f32[10,1024,128]{2,1,0:T(8,128)} %bitcast.19), custom_call_target="tpu_custom_call" | custom-call | tf_op jit(solution)/shard_map/cross/pallas_call | solution.py:86
  52.6 5.4 %all-to-all-done.1 = f32[32,8,256]{2,1,0:T(8,128)S(1)} async-done(((f32[32,8,256]{2,1,0:T(8,128)}), f32[32,8,256]{2,1,0:T(8,128)S(1)}, u32[]{:S(2)}, u32[]{:S(2)}) %all-to-all-start.1) | async-done | bytes 262176 | tf_op jit(solution)/shard_map/all_to_all | solution.py:273
  58.0 4.3 %all-to-all-start.2 = ((f32[4,64,1280]{2,1,0:T(8,128)}), f32[4,64,1280]{2,1,0:T(8,128)}, u32[]{:S(2)}, u32[]{:S(2)}) async-start(f32[4,64,1280]{2,1,0:T(8,128)} %bitcast.5), calls=%async_computation.2 | async-start | bytes 2621440 | tf_op jit(solution)/shard_map/all_to_all | solution.py:266
  62.3 0.7 collective-permute-start.7
  62.9 0.7 collective-permute-start.6
  63.6 1.3 collective-permute-start.5
  64.9 0.0 collective-permute-done.7.refs_3_
  64.9 0.0 collective-permute-done.6.refs_2_
  65.0 10.1 %collective-permute-done.5.refs_1_ = f32[256,256]{1,0:T(8,128)S(1)} collective-permute-done((f32[256,256]{1,0:T(8,128)S(1)}, f32[256,256]{1,0:T(8,128)S(1)}, u32[]{:S(2)}, u32[]{:S(2)}) %collective-permute-start.5) | collective-permute-done | bytes 262176 | tf_op jit(solution)/shard_map/ppermute | solution.py:27
  75.0 6.5 %factor_first.1 = (f32[128,128]{1,0:T(8,128)S(1)}, f32[128,128]{1,0:T(8,128)S(1)}, f32[128,128]{1,0:T(8,128)S(1)}) custom-call(s32[1]{0:T(128)} %bitcast.6.x_ref, f32[256,256]{1,0:T(8,128)S(1)} %bitcast.17, f32[256,256]{1,0:T(8,128)S(1)} %collective-permute-done.5.refs_1_, f32[256,256]{1,0:T(8,128)S(1)} %collective-permute-done.6.refs_2_, ...), custom_call_target="tpu_custom_call" | custom-call | tf_op jit(solution)/shard_map/factor_first/pallas_call | solution.py:204
  81.5 0.0 all-to-all-done.2
  81.6 2.1 %reduce_sum.28 = f32[64,1280]{1,0:T(8,128)} reduce(f32[4,64,1280]{2,1,0:T(8,128)} %all-to-all-done.2, f32[]{:T(128)} %constant.3.clone.1), dimensions={0}, to_apply=%region_1.2 | reduce | flops 245760 | bytes 1638404 | tf_op jit(solution)/shard_map/reduce_sum | solution.py:267
  83.7 3.6 %all-to-all-start.3 = ((f32[8,8,1280]{2,1,0:T(8,128)}), f32[8,8,1280]{2,1,0:T(8,128)S(1)}, u32[]{:S(2)}, u32[]{:S(2)}) async-start(f32[8,8,1280]{2,1,0:T(8,128)} %bitcast.7), calls=%async_computation.3 | async-start | bytes 655360 | tf_op jit(solution)/shard_map/all_to_all | solution.py:266
  87.3 7.1 %factor_last.1 = (f32[256,256]{1,0:T(8,128)S(1)}, f32[1024,256]{1,0:T(8,128)S(1)}) custom-call(f32[128,128]{1,0:T(8,128)S(1)} %get-tuple-element.37.w11_ref, f32[128,128]{1,0:T(8,128)S(1)} %get-tuple-element.38.l_ref, f32[128,128]{1,0:T(8,128)S(1)} %get-tuple-element.39.s_ref, f32[1024,256]{1,0:T(8,128)S(1)} %get-tuple-element.40.p_ref), custom_call_target="tpu_custom_call" | custom-call | tf_op jit(solution)/shard_map/factor_last/pallas_call | solution.py:219
  94.4 5.2 %all-to-all-done.3 = f32[8,8,1280]{2,1,0:T(8,128)S(1)} async-done(((f32[8,8,1280]{2,1,0:T(8,128)}), f32[8,8,1280]{2,1,0:T(8,128)S(1)}, u32[]{:S(2)}, u32[]{:S(2)}) %all-to-all-start.3) | async-done | bytes 327712 | tf_op jit(solution)/shard_map/all_to_all | solution.py:266
  99.7 14.1 %all_to_all.30 = f32[8,8,1280]{2,1,0:T(8,128)S(1)} all-to-all(f32[8,8,1280]{2,1,0:T(8,128)S(1)} %broadcast_in_dim.29), channel_id=1, replica_groups=mesh['z'=8,'y'=4,'x'=4,'c'=2] {'z'}, dimensions={0} | all-to-all | bytes 655360 | tf_op jit(solution)/shard_map/all_to_all | solution.py:273
  113.8 0.1 broadcast_in_dim.31
  113.9 17.8 %all_to_all.31 = f32[4,64,1280]{2,1,0:T(8,128)S(1)} all-to-all(f32[4,64,1280]{2,1,0:T(8,128)S(1)} %broadcast_in_dim.31), channel_id=1, replica_groups=mesh['z'=8,'y'=4,'x'=4,'c'=2] {'y'}, dimensions={0} | all-to-all | bytes 2621440 | tf_op jit(solution)/shard_map/all_to_all | solution.py:273
  131.6 11.0 %update.1 = (f32[10,1024,128]{2,1,0:T(8,128)}, f32[10,256,128]{2,1,0:T(8,128)}) custom-call(f32[256,256]{1,0:T(8,128)S(1)} %get-tuple-element.43.w_ref, f32[256,1280]{1,0:T(8,128)S(1)} %bitcast.13, f32[1024,256]{1,0:T(8,128)S(1)} %get-tuple-element.45.q_ref, f32[10,1024,128]{2,1,0:T(8,128)} %bitcast.20), custom_call_target="tpu_custom_call" | custom-call | tf_op jit(solution)/shard_map/update/pallas_call | solution.py:242
  (3 shorter events, 0.1 us)
Async XLA Ops:
  1.7 2.8 %collective-permute-start = (f32[1024,128]{1,0:T(8,128)S(1)}, f32[1024,128]{1,0:T(8,128)S(1)}, u32[]{:S(2)}, u32[]{:S(2)}) collective-permute-start(f32[1024,128]{1,0:T(8,128)S(1)} %slice_bitcast_fusion.mine_ref), channel_id=1, source_target_pairs={{0,1},{1,0},{2,3},{3,2},{4,5},{5,4},{6,7},{7,6},{8,9},{9,8},{10,11... | collective-permute-start | bytes 1572872 | tf_op jit(solution)/shard_map/ppermute | solution.py:31
  1.8 29.9 %collective-permute-start.3 = (f32[1024,128]{1,0:T(8,128)S(1)}, f32[1024,128]{1,0:T(8,128)S(1)}, u32[]{:S(2)}, u32[]{:S(2)}) collective-permute-start(f32[1024,128]{1,0:T(8,128)S(1)} %slice_bitcast_fusion.mine_ref), channel_id=1, source_target_pairs={{0,6},{1,7},{8,14},{9,15},{16,22},{17,23},{24,30},{25,31},{32,38},... | collective-permute-start | bytes 1572872 | tf_op jit(solution)/shard_map/ppermute | solution.py:27
  2.5 29.2 %collective-permute-start.2 = (f32[1024,128]{1,0:T(8,128)S(1)}, f32[1024,128]{1,0:T(8,128)S(1)}, u32[]{:S(2)}, u32[]{:S(2)}) collective-permute-start(f32[1024,128]{1,0:T(8,128)S(1)} %slice_bitcast_fusion.mine_ref), channel_id=1, source_target_pairs={{0,4},{1,5},{8,12},{9,13},{16,20},{17,21},{24,28},{25,29},{32,36},... | collective-permute-start | bytes 1572872 | tf_op jit(solution)/shard_map/ppermute | solution.py:27
  3.2 28.6 %collective-permute-start.1 = (f32[1024,128]{1,0:T(8,128)S(1)}, f32[1024,128]{1,0:T(8,128)S(1)}, u32[]{:S(2)}, u32[]{:S(2)}) collective-permute-start(f32[1024,128]{1,0:T(8,128)S(1)} %slice_bitcast_fusion.mine_ref), channel_id=1, source_target_pairs={{0,2},{1,3},{8,10},{9,11},{16,18},{17,19},{24,26},{25,27},{32,34},... | collective-permute-start | bytes 1572872 | tf_op jit(solution)/shard_map/ppermute | solution.py:27
  6.4 25.2 %all-to-all-start = ((f32[32,8,256]{2,1,0:T(8,128)}), f32[32,8,256]{2,1,0:T(8,128)S(1)}, u32[]{:S(2)}, u32[]{:S(2)}) async-start(f32[32,8,256]{2,1,0:T(8,128)} %bitcast.3), calls=%async_computation | async-start | bytes 524288 | tf_op jit(solution)/shard_map/all_to_all | solution.py:266
  31.9 12.3 %collective-permute-start.4 = (f32[1024,128]{1,0:T(8,128)S(1)}, f32[1024,128]{1,0:T(8,128)S(1)}, u32[]{:S(2)}, u32[]{:S(2)}) collective-permute-start(f32[1024,128]{1,0:T(8,128)S(1)} %select_select_fusion.mine_ref), channel_id=1, source_target_pairs={{0,1},{1,0},{2,3},{3,2},{4,5},{5,4},{6,7},{7,6},{8,9},{9,8},{10,11... | collective-permute-start | bytes 1572872 | tf_op jit(solution)/shard_map/ppermute | solution.py:31
  32.8 25.2 %all-to-all-start.1 = ((f32[32,8,256]{2,1,0:T(8,128)}), f32[32,8,256]{2,1,0:T(8,128)S(1)}, u32[]{:S(2)}, u32[]{:S(2)}) async-start(f32[32,8,256]{2,1,0:T(8,128)} %broadcast_in_dim.13), calls=%async_computation.1 | async-start | bytes 524288 | tf_op jit(solution)/shard_map/all_to_all | solution.py:273
  58.0 23.6 %all-to-all-start.2 = ((f32[4,64,1280]{2,1,0:T(8,128)}), f32[4,64,1280]{2,1,0:T(8,128)}, u32[]{:S(2)}, u32[]{:S(2)}) async-start(f32[4,64,1280]{2,1,0:T(8,128)} %bitcast.5), calls=%async_computation.2 | async-start | bytes 2621440 | tf_op jit(solution)/shard_map/all_to_all | solution.py:266
  62.3 2.7 %collective-permute-start.7 = (f32[256,256]{1,0:T(8,128)S(1)}, f32[256,256]{1,0:T(8,128)S(1)}, u32[]{:S(2)}, u32[]{:S(2)}) collective-permute-start(f32[256,256]{1,0:T(8,128)S(1)} %bitcast.14), channel_id=1, source_target_pairs={{0,6},{1,7},{8,14},{9,15},{16,22},{17,23},{24,30},{25,31},{32,38},... | collective-permute-start | bytes 786440 | tf_op jit(solution)/shard_map/ppermute | solution.py:27
  62.9 2.0 %collective-permute-start.6 = (f32[256,256]{1,0:T(8,128)S(1)}, f32[256,256]{1,0:T(8,128)S(1)}, u32[]{:S(2)}, u32[]{:S(2)}) collective-permute-start(f32[256,256]{1,0:T(8,128)S(1)} %bitcast.15), channel_id=1, source_target_pairs={{0,4},{1,5},{8,12},{9,13},{16,20},{17,21},{24,28},{25,29},{32,36},... | collective-permute-start | bytes 786440 | tf_op jit(solution)/shard_map/ppermute | solution.py:27
  63.6 11.4 %collective-permute-start.5 = (f32[256,256]{1,0:T(8,128)S(1)}, f32[256,256]{1,0:T(8,128)S(1)}, u32[]{:S(2)}, u32[]{:S(2)}) collective-permute-start(f32[256,256]{1,0:T(8,128)S(1)} %bitcast.16), channel_id=1, source_target_pairs={{0,2},{1,3},{8,10},{9,11},{16,18},{17,19},{24,26},{25,27},{32,34},... | collective-permute-start | bytes 786440 | tf_op jit(solution)/shard_map/ppermute | solution.py:27
  83.7 15.9 %all-to-all-start.3 = ((f32[8,8,1280]{2,1,0:T(8,128)}), f32[8,8,1280]{2,1,0:T(8,128)S(1)}, u32[]{:S(2)}, u32[]{:S(2)}) async-start(f32[8,8,1280]{2,1,0:T(8,128)} %bitcast.7), calls=%async_computation.3 | async-start | bytes 655360 | tf_op jit(solution)/shard_map/all_to_all | solution.py:266

commit v4 on v2

--- a/solution.py
+++ b/solution.py
@@ -8,8 +8,9 @@
 PRECISE = lax.Precision.HIGHEST
 NZ, NY, NX, NC = 8, 4, 4, 2
 LANES, SUB = 128, 8
+RIDE = 1280
 NT = (((1,), (1,)), ((), ()))
-VMEM_BYTES = 48 << 20
+PARAMS = pltpu.CompilerParams(vmem_limit_bytes=48 << 20)
 
 
 def dot(left, right, dims=(((1,), (0,)), ((), ()))):
@@ -21,6 +22,10 @@
     for at in range(len(choices) - 2, -1, -1):
         value = jnp.where(index == at, choices[at], value)
     return value
+
+
+def swap(values):
+    return lax.ppermute(values, "c", [(0, 1), (1, 0)])
 
 
 def relay(own):
@@ -35,49 +40,119 @@
     on_high = lax.ppermute(down_high, "x", [(3, 2)])
     mine_low = pick(x, [low, up_low, on_low, down_low])
     mine_high = pick(x, [high, up_high, on_high, down_high])
-    swap = [(0, 1), (1, 0)]
-    return mine_low, mine_high, lax.ppermute(mine_low, "c", swap), lax.ppermute(mine_high, "c", swap)
-
-
-def products_kernel(core_ref, ml_ref, mh_ref, ol_ref, oh_ref, c_ref, o_ref, p_ref, pt_ref):
+    return mine_low, mine_high, swap(mine_low), swap(mine_high)
+
+
+def index_of(axis):
+    return lax.axis_index(axis).astype(jnp.int32)[None]
+
+
+SCALAR = pl.BlockSpec(memory_space=pltpu.SMEM)
+
+
+def whole(shape):
+    return pl.BlockSpec(shape, lambda i: (0,) * len(shape))
+
+
+def place(core, pieces, p_ref):
+    half, k = pieces[0].shape
+    first = core == 0
+    for at in range(2):
+        rows = slice(at * half, (at + 1) * half)
+        mine, other = pieces[at][...], pieces[2 + at][...]
+        p_ref[rows, :k] = jnp.where(first, mine, other)
+        p_ref[rows, k:] = jnp.where(first, other, mine)
+
+
+def products_kernel(x_ref, core_ref, ml_ref, mh_ref, ol_ref, oh_ref, c_ref, o_ref, p_ref, pt_ref):
     i = pl.program_id(0)
-    half, k = ml_ref.shape
+    k = c_ref.shape[2]
+    w = 2 * k
 
     @pl.when(i == 0)
     def _():
-        first = core_ref[0] == 0
-        for rows, m_ref, t_ref in ((slice(0, half), ml_ref, ol_ref), (slice(half, 2 * half), mh_ref, oh_ref)):
-            mine, other = m_ref[...], t_ref[...]
-            p_ref[rows, :k] = jnp.where(first, mine, other)
-            p_ref[rows, k:] = jnp.where(first, other, mine)
+        place(core_ref[0], (ml_ref, mh_ref, ol_ref, oh_ref), p_ref)
         pt_ref[...] = p_ref[...].T
-        o_ref[...] = dot(pt_ref[...], p_ref[...])
-
-    @pl.when(i > 0)
-    def _():
-        o_ref[...] = dot(pt_ref[...], jnp.concatenate([c_ref[0], c_ref[1]], axis=1))
+        share = NY * SUB
+        at = pl.multiple_of((x_ref[0] * NC + core_ref[0]) * share, share)
+        gram = dot(pt_ref[pl.ds(at, share), :], p_ref[...])
+        o_ref[:, RIDE:] = jnp.zeros((w, LANES), jnp.float32)
+        for y in range(NY):
+            row = y * (w // NY)
+            piece = gram[y * SUB : (y + 1) * SUB]
+            o_ref[row : row + SUB, RIDE:] = piece[:, :LANES]
+            o_ref[row + SUB : row + 2 * SUB, RIDE:] = piece[:, LANES:]
+
+    lanes = pl.ds(pl.multiple_of(i * w, w), w)
+    o_ref[:, lanes] = dot(pt_ref[...], jnp.concatenate([c_ref[0], c_ref[1]], axis=1))
 
 
 def products(pieces, columns):
     rounds, n, k = columns.shape
     w = 2 * k
-    core = lax.axis_index("c").astype(jnp.int32)[None]
-    whole = pl.BlockSpec((n // 2, k), lambda i: (0, 0))
     return pl.pallas_call(
         products_kernel,
-        grid=(rounds // 2 + 1,),
-        in_specs=[pl.BlockSpec(memory_space=pltpu.SMEM)]
-        + [whole] * 4
-        + [pl.BlockSpec((2, n, k), lambda i: (jnp.maximum(i - 1, 0), 0, 0))],
-        out_specs=[pl.BlockSpec((w, w), lambda i: (0, i)), pl.BlockSpec((n, w), lambda i: (0, 0))],
+        grid=(rounds // 2,),
+        in_specs=[SCALAR, SCALAR]
+        + [whole((n // 2, k))] * 4
+        + [pl.BlockSpec((2, n, k), lambda i: (i, 0, 0))],
+        out_specs=[whole((w, RIDE + LANES)), whole((n, w))],
         out_shape=[
-            jax.ShapeDtypeStruct((w, w + rounds * k), jnp.float32),
+            jax.ShapeDtypeStruct((w, RIDE + LANES), jnp.float32),
             jax.ShapeDtypeStruct((n, w), jnp.float32),
         ],
         scratch_shapes=[pltpu.VMEM((w, n), jnp.float32)],
-        compiler_params=pltpu.CompilerParams(vmem_limit_bytes=VMEM_BYTES),
+        compiler_params=PARAMS,
         name="products",
-    )(core, *pieces, columns)
+    )(index_of("x"), index_of("c"), *pieces, columns)
+
+
+def sum_y_kernel(a_ref, o_ref):
+    total = (a_ref[0] + a_ref[1]) + (a_ref[2] + a_ref[3])
+    for z in range(NZ):
+        o_ref[z, :, :RIDE] = total[z * SUB : (z + 1) * SUB, :RIDE]
+        o_ref[z, :, RIDE : RIDE + LANES] = total[:SUB, RIDE:]
+        o_ref[z, :, RIDE + LANES :] = total[SUB : 2 * SUB, RIDE:]
+
+
+def sum_y(pieces):
+    out = (NZ, SUB, RIDE + 2 * LANES)
+    return pl.pallas_call(
+        sum_y_kernel,
+        grid=(1,),
+        in_specs=[whole(pieces.shape)],
+        out_specs=whole(out),
+        out_shape=jax.ShapeDtypeStruct(out, jnp.float32),
+        compiler_params=PARAMS,
+        name="sum_y",
+    )(pieces)
+
+
+def sum_z_kernel(a_ref, o_ref, g_ref):
+    total = a_ref[0]
+    for z in range(1, NZ):
+        total = total + a_ref[z]
+    for z in range(NZ):
+        o_ref[z] = total[:, :RIDE]
+    g_ref[...] = total[:, RIDE:]
+
+
+def sum_z(pieces):
+    copies, gram = (NZ, SUB, RIDE), (SUB, 2 * LANES)
+    return pl.pallas_call(
+        sum_z_kernel,
+        grid=(1,),
+        in_specs=[whole(pieces.shape)],
+        out_specs=[whole(copies), whole(gram)],
+        out_shape=[jax.ShapeDtypeStruct(copies, jnp.float32), jax.ShapeDtypeStruct(gram, jnp.float32)],
+        compiler_params=PARAMS,
+        name="sum_z",
+    )(pieces)
+
+
+def collect(values, axis, size):
+    hops = [[(at, (at - by) % size) for at in range(size)] for by in range(1, size)]
+    return jnp.concatenate([values] + [lax.ppermute(values, axis, pairs) for pairs in hops], axis=0)
 
 
 def inverse_root(d):
@@ -155,33 +230,58 @@
             w_ref[row0 + j + k:row0 + j + k + 1, col0:col0 + LANES] = w[0:1]
 
 
-def factor_kernel(y_ref, g0_ref, g1_ref, g2_ref, g3_ref, p_ref, w_ref, q_ref, g_ref):
-    part, h = g0_ref.shape[0], LANES
-    y = y_ref[0]
-    for step, block in enumerate((g0_ref, g1_ref, g2_ref, g3_ref)):
-        at = pl.multiple_of(((y + step) % NY) * part, part)
-        g_ref[pl.ds(at, part), :] = block[...]
+def factor_first_kernel(x_ref, y_ref, core_ref, mine_ref, other_ref, w_ref, l_ref, s_ref, g_ref):
+    h = LANES
+    for half, half_ref in enumerate((mine_ref, other_ref)):
+        core = (core_ref[0] + half) % NC
+        for dy in range(NY):
+            for dx in range(NX):
+                x, y = (x_ref[0] + dx) % NX, (y_ref[0] + dy) % NY
+                at = pl.multiple_of(((x * NC + core) * NY + y) * SUB, SUB)
+                row = (dy * NX + dx) * SUB
+                g_ref[pl.ds(at, SUB), :] = half_ref[row : row + SUB, :]
     invert_factor(g_ref[:h, :h], w_ref, 0, 0)
+    l21 = dot(g_ref[h:, :h], w_ref[...], NT)
+    l_ref[...] = l21
+    s_ref[...] = g_ref[h:, h:] - dot(l21, l21, NT)
+
+
+def factor_last_kernel(w11_ref, l_ref, s_ref, p_ref, w_ref, q_ref):
+    h = LANES
+    w11 = w11_ref[...]
+    w_ref[:h, :h] = w11
     w_ref[:h, h:] = jnp.zeros((h, h), jnp.float32)
-    w11 = w_ref[:h, :h]
-    l21 = dot(g_ref[h:, :h], w11, NT)
-    invert_factor(g_ref[h:, h:] - dot(l21, l21, NT), w_ref, h, h)
-    w_ref[h:, :h] = -dot(w_ref[h:, h:], dot(l21, w11))
+    invert_factor(s_ref[...], w_ref, h, h)
+    w_ref[h:, :h] = -dot(w_ref[h:, h:], dot(l_ref[...], w11))
     q_ref[...] = dot(p_ref[...], w_ref[...], NT)
 
 
-def factor(parts, panels):
+def factor_first(mine, other):
+    h, w = mine.shape
+    return pl.pallas_call(
+        factor_first_kernel,
+        grid=(1,),
+        in_specs=[SCALAR] * 3 + [whole((h, w))] * 2,
+        out_specs=[whole((h, h))] * 3,
+        out_shape=[jax.ShapeDtypeStruct((h, h), jnp.float32)] * 3,
+        scratch_shapes=[pltpu.VMEM((w, w), jnp.float32)],
+        compiler_params=PARAMS,
+        name="factor_first",
+    )(index_of("x"), index_of("y"), index_of("c"), mine, other)
+
+
+def factor_last(w11, l21, schur, panels):
     n, w = panels.shape
-    y = lax.axis_index("y").astype(jnp.int32)[None]
-    vmem = pl.BlockSpec(memory_space=pltpu.VMEM)
-    return pl.pallas_call(
-        factor_kernel,
-        in_specs=[pl.BlockSpec(memory_space=pltpu.SMEM)] + [vmem] * 5,
+    h = w // 2
+    return pl.pallas_call(
+        factor_last_kernel,
+        grid=(1,),
+        in_specs=[whole((h, h))] * 3 + [whole((n, w))],
+        out_specs=[whole((w, w)), whole((n, w))],
         out_shape=[jax.ShapeDtypeStruct((w, w), jnp.float32), jax.ShapeDtypeStruct((n, w), jnp.float32)],
-        scratch_shapes=[pltpu.VMEM((w, w), jnp.float32)],
-        compiler_params=pltpu.CompilerParams(vmem_limit_bytes=VMEM_BYTES),
-        name="factor",
-    )(y, *parts, panels)
+        compiler_params=PARAMS,
+        name="factor_last",
+    )(w11, l21, schur, panels)
 
 
 def update_kernel(w_ref, x_ref, q_ref, c_ref, red_ref, top_ref):
@@ -213,34 +313,27 @@
             jax.ShapeDtypeStruct((rounds, n, k), jnp.float32),
             jax.ShapeDtypeStruct((rounds, w, k), jnp.float32),
         ],
-        compiler_params=pltpu.CompilerParams(vmem_limit_bytes=VMEM_BYTES),
+        compiler_params=PARAMS,
         name="update",
     )(inverse, cross, basis, columns)
 
 
-def scatter_sum(values, axis, parts):
-    rows, width = values.shape
-    pieces = lax.all_to_all(values.reshape(parts, rows // parts, width), axis, 0, 0)
-    return jnp.sum(pieces, axis=0)
-
-
-def gather(values, axis, parts):
-    rows, width = values.shape
-    copies = jnp.broadcast_to(values[None], (parts, rows, width))
-    return lax.all_to_all(copies, axis, 0, 0).reshape(parts * rows, width)
+def exchange(pieces, axis):
+    return lax.all_to_all(pieces, axis, 0, 0)
 
 
 def shards(matrix):
+    hold = lax.optimization_barrier
     columns = jnp.transpose(matrix, (1, 0, 2))
     both, panels = products(relay(columns[0]), columns)
-    part = scatter_sum(both, "y", NY)
-    part = scatter_sum(part, "z", NZ)
-    part = gather(part, "z", NZ)
     w = panels.shape[1]
-    gram_part, cross_part = part[:, :w], part[:, w:]
-    ahead = [lax.ppermute(gram_part, "y", [(y, (y - by) % NY) for y in range(NY)]) for by in (1, 2, 3)]
-    inverse, basis = factor([gram_part, *ahead], panels)
-    cross = gather(cross_part, "y", NY)
+    pieces = sum_y(exchange(both.reshape(NY, w // NY, RIDE + LANES), "y"))
+    copies, gram = sum_z(exchange(pieces, "z"))
+    part = exchange(copies, "z").reshape(w // NY, RIDE)
+    gram = collect(collect(gram, "x", NX), "y", NY)
+    part, gram = hold((part, gram))
+    inverse, basis = factor_last(*factor_first(gram, swap(gram)), panels)
+    cross = exchange(jnp.broadcast_to(part[None], (NY, w // NY, RIDE)), "y").reshape(w, RIDE)
     reduced, top = update(inverse, basis, cross, columns)
     return jnp.transpose(reduced, (1, 0, 2)), jnp.transpose(top, (1, 0, 2))
 

time: 150 us -> 134 us (0.89)
  the two profiles are of different devices: /device:TPU:4 before, /device:TPU:8 now
where the time goes in v4:
time: 134 us; the launch traced here: 132 us
  blocking collectives  44.7 us (33%)
  Pallas kernels  33.5 us (25%)
  starting transfers between devices  32 us (24%)
  waiting for transfers between devices  16.2 us (12%)
  local copies, waits for them, and re-layouts  3.9 us (3%)
    all_to_all x2, blocking collectives, exchange(): return lax.all_to_all(pieces, axis, 0, 0)  44.7 us
    ppermute x6, starting transfers between devices, collect(): lax.ppermute(values, axis, pairs)  13.1 us
    pallas_call x1, Pallas kernels, update(): pl.pallas_call(update_kernel, grid=(rounds // 2,), in_specs=[pl.BlockSpec...  11 us
    all_to_all x2, starting transfers between devices, exchange(): return lax.all_to_all(pieces, axis, 0, 0)  8.4 us
    pallas_call x1, Pallas kernels, products(): pl.pallas_call(products_kernel, grid=(rounds // 2,), in_specs=[SCALAR, SC...  8.04 us
    pallas_call x1, Pallas kernels, factor_last(): pl.pallas_call(factor_last_kernel, grid=(1,), in_specs=[whole((h, h))] *...  7.06 us
    pallas_call x1, Pallas kernels, factor_first(): pl.pallas_call(factor_first_kernel, grid=(1,), in_specs=[SCALAR] * 3 + [w...  6.58 us
    ppermute x1, starting transfers between devices, relay(): down_high = lax.ppermute(high, 'x', [(0, 3)])  4.68 us
  transfers between devices with their start and end apart: 17, of which 8 were waited for; matrix products, arithmetic and copies ran while one was open for 0% of the time, Pallas kernels for 10%

profile of v4, /device:TPU:8, one launch (start us, length us, event | category | flops | bytes accessed | tf_op | source)
XLA Modules:
  0.0 132.1 jit_solution(5808611385617793229)
XLA Ops:
  0.6 1.1 slice_bitcast_fusion
  1.7 4.7 %collective-permute-start.4 = (f32[512,128]{1,0:T(8,128)S(1)}, f32[512,128]{1,0:T(8,128)S(1)}, u32[]{:S(2)}, u32[]{:S(2)}) collective-permute-start(f32[512,128]{1,0:T(8,128)S(1)} %get-tuple-element.30), channel_id=1, source_target_pairs={{0,6},{1,7},{8,14},{9,15},{16,22},{17,23},{24,30},{25,31},{32,38},... | collective-permute-start | bytes 786440 | tf_op jit(solution)/shard_map/ppermute | solution.py:36
  6.4 1.3 collective-permute-start
  7.7 1.3 collective-permute-start.3
  9.0 1.3 collective-permute-start.2
  10.3 2.7 %collective-permute-done.4 = f32[512,128]{1,0:T(8,128)S(1)} collective-permute-done((f32[512,128]{1,0:T(8,128)S(1)}, f32[512,128]{1,0:T(8,128)S(1)}, u32[]{:S(2)}, u32[]{:S(2)}) %collective-permute-start.4) | collective-permute-done | bytes 262176 | tf_op jit(solution)/shard_map/ppermute | solution.py:36
  13.1 0.7 collective-permute-start.5
  13.7 0.6 collective-permute-done
  14.4 0.7 collective-permute-start.1
  15.1 3.8 %collective-permute-done.3 = f32[512,128]{1,0:T(8,128)S(1)} collective-permute-done((f32[512,128]{1,0:T(8,128)S(1)}, f32[512,128]{1,0:T(8,128)S(1)}, u32[]{:S(2)}, u32[]{:S(2)}) %collective-permute-start.3) | collective-permute-done | bytes 262176 | tf_op jit(solution)/shard_map/ppermute | solution.py:37
  18.8 0.0 collective-permute-done.2
  18.9 0.0 collective-permute-done.5
  18.9 0.0 collective-permute-done.1
  18.9 1.1 select_select_fusion
  20.0 0.1 collective-permute-start.7
  20.1 0.5 collective-permute-start.6
  20.6 1.0 collective-permute-done.7.oh_ref
  21.6 0.4 collective-permute-done.6.ol_ref
  22.0 8.0 %products.1 = (f32[256,1408]{1,0:T(8,128)S(1)}, f32[1024,256]{1,0:T(8,128)S(1)}) custom-call(s32[1]{0:T(128)} %bitcast.x_ref, s32[1]{0:T(128)} %bitcast.2.core_ref, f32[512,128]{1,0:T(8,128)S(1)} %get-tuple-element.29.ml_ref, f32[512,128]{1,0:T(8,128)S(1)} %get-tuple-element.28.mh_ref, f32[512,128]{1,0:T(8,128)S(1)} %collective-permute-done.6.ol_ref, ...), custom_call_target="tpu_custom_call" | custom-call | tf_op jit(solution)/shard_map/products/pallas_call | solution.py:93
  30.0 22.9 %all_to_all.20.a_ref = f32[4,64,1408]{2,1,0:T(8,128)S(1)} all-to-all(f32[4,64,1408]{2,1,0:T(8,128)S(1)} %bitcast.18), channel_id=1, replica_groups=mesh['z'=8,'y'=4,'x'=4,'c'=2] {'y'}, dimensions={0} | all-to-all | bytes 2883584 | tf_op jit(solution)/shard_map/all_to_all | solution.py:322
  52.9 0.1 sum_y.1
  53.0 21.8 %all_to_all.21.a_ref = f32[8,8,1536]{2,1,0:T(8,128)S(1)} all-to-all(f32[8,8,1536]{2,1,0:T(8,128)S(1)} %sum_y.1), channel_id=1, replica_groups=mesh['z'=8,'y'=4,'x'=4,'c'=2] {'z'}, dimensions={0} | all-to-all | bytes 786432 | tf_op jit(solution)/shard_map/all_to_all | solution.py:322
  74.8 0.8 sum_z.1
  75.5 3.1 %collective-permute-start.10 = (f32[8,256]{1,0:T(8,128)S(1)}, f32[8,256]{1,0:T(8,128)S(1)}, u32[]{:S(2)}, u32[]{:S(2)}) collective-permute-start(f32[8,256]{1,0:T(8,128)S(1)} %get-tuple-element.17), channel_id=1, source_target_pairs={{0,2},{2,4},{4,6},{6,0},{1,3},{3,5},{5,7},{7,1},{8,10},{10,12},{12... | collective-permute-start | bytes 24584 | tf_op jit(solution)/shard_map/ppermute | solution.py:155
  78.7 2.5 %collective-permute-start.9 = (f32[8,256]{1,0:T(8,128)S(1)}, f32[8,256]{1,0:T(8,128)S(1)}, u32[]{:S(2)}, u32[]{:S(2)}) collective-permute-start(f32[8,256]{1,0:T(8,128)S(1)} %get-tuple-element.17), channel_id=1, source_target_pairs={{0,4},{2,6},{4,0},{6,2},{1,5},{3,7},{5,1},{7,3},{8,12},{10,14},{12... | collective-permute-start | bytes 24584 | tf_op jit(solution)/shard_map/ppermute | solution.py:155
  81.2 2.6 %collective-permute-start.8 = (f32[8,256]{1,0:T(8,128)S(1)}, f32[8,256]{1,0:T(8,128)S(1)}, u32[]{:S(2)}, u32[]{:S(2)}) collective-permute-start(f32[8,256]{1,0:T(8,128)S(1)} %get-tuple-element.17), channel_id=1, source_target_pairs={{0,6},{2,0},{4,2},{6,4},{1,7},{3,1},{5,3},{7,5},{8,14},{10,8},{12,... | collective-permute-start | bytes 24584 | tf_op jit(solution)/shard_map/ppermute | solution.py:155
  83.8 3.4 %all-to-all-start.2 = ((f32[8,8,1280]{2,1,0:T(8,128)}), f32[8,8,1280]{2,1,0:T(8,128)S(1)}, u32[]{:S(2)}, u32[]{:S(2)}) async-start(f32[8,8,1280]{2,1,0:T(8,128)} %get-tuple-element.16), calls=%async_computation.2 | async-start | bytes 655360 | tf_op jit(solution)/shard_map/all_to_all | solution.py:322
  87.3 0.0 collective-permute-done.8
  87.3 0.0 collective-permute-done.9
  87.3 0.0 collective-permute-done.10
  87.4 1.5 %collective-permute-start.11 = (f32[32,256]{1,0:T(8,128)S(1)}, f32[32,256]{1,0:T(8,128)S(1)}, u32[]{:S(2)}, u32[]{:S(2)}) collective-permute-start(f32[32,256]{1,0:T(8,128)S(1)} %get-tuple-element.32), channel_id=1, source_target_pairs={{0,24},{8,0},{16,8},{24,16},{1,25},{9,1},{17,9},{25,17},{2,26},{10... | collective-permute-start | bytes 98312 | tf_op jit(solution)/shard_map/ppermute | solution.py:155
  88.9 0.6 collective-permute-start.13
  89.5 2.7 %collective-permute-start.12 = (f32[32,256]{1,0:T(8,128)S(1)}, f32[32,256]{1,0:T(8,128)S(1)}, u32[]{:S(2)}, u32[]{:S(2)}) collective-permute-start(f32[32,256]{1,0:T(8,128)S(1)} %get-tuple-element.32), channel_id=1, source_target_pairs={{0,16},{8,24},{16,0},{24,8},{1,17},{9,25},{17,1},{25,9},{2,18},{10... | collective-permute-start | bytes 98312 | tf_op jit(solution)/shard_map/ppermute | solution.py:155
  92.1 0.0 collective-permute-done.11
  92.1 2.7 %collective-permute-done.12 = f32[32,256]{1,0:T(8,128)S(1)} collective-permute-done((f32[32,256]{1,0:T(8,128)S(1)}, f32[32,256]{1,0:T(8,128)S(1)}, u32[]{:S(2)}, u32[]{:S(2)}) %collective-permute-start.12) | collective-permute-done | bytes 32800 | tf_op jit(solution)/shard_map/ppermute | solution.py:155
  94.9 0.0 collective-permute-done.13
  94.9 3.5 %all-to-all-done.2 = f32[8,8,1280]{2,1,0:T(8,128)S(1)} async-done(((f32[8,8,1280]{2,1,0:T(8,128)}), f32[8,8,1280]{2,1,0:T(8,128)S(1)}, u32[]{:S(2)}, u32[]{:S(2)}) %all-to-all-start.2) | async-done | bytes 327712 | tf_op jit(solution)/shard_map/all_to_all | solution.py:322
  98.4 1.2 broadcast_in_dim.20
  99.5 5.0 %all-to-all-start.3 = ((f32[4,64,1280]{2,1,0:T(8,128)}), f32[4,64,1280]{2,1,0:T(8,128)S(1)}, u32[]{:S(2)}, u32[]{:S(2)}) async-start(f32[4,64,1280]{2,1,0:T(8,128)} %broadcast_in_dim.20), calls=%async_computation.3 | async-start | bytes 2621440 | tf_op jit(solution)/shard_map/all_to_all | solution.py:322
  104.5 0.0 collective-permute-start.14
  104.5 1.3 %collective-permute-done.14.other_ref = f32[128,256]{1,0:T(8,128)S(1)} collective-permute-done((f32[128,256]{1,0:T(8,128)S(1)}, f32[128,256]{1,0:T(8,128)S(1)}, u32[]{:S(2)}, u32[]{:S(2)}) %collective-permute-start.14) | collective-permute-done | bytes 131104 | tf_op jit(solution)/shard_map/ppermute | solution.py:28
  105.8 6.6 %factor_first.1 = (f32[128,128]{1,0:T(8,128)S(1)}, f32[128,128]{1,0:T(8,128)S(1)}, f32[128,128]{1,0:T(8,128)S(1)}) custom-call(s32[1]{0:T(128)} %bitcast.x_ref, s32[1]{0:T(128)} %bitcast.1.y_ref, s32[1]{0:T(128)} %bitcast.2.core_ref, f32[128,256]{1,0:T(8,128)S(1)} %constant_dynamic-update-slice_fusion.4.mine_ref, ...), custom_call_target="tpu_custom_call" | custom-call | tf_op jit(solution)/shard_map/factor_first/pallas_call | solution.py:261
  112.4 7.1 %factor_last.1 = (f32[256,256]{1,0:T(8,128)S(1)}, f32[1024,256]{1,0:T(8,128)S(1)}) custom-call(f32[128,128]{1,0:T(8,128)S(1)} %get-tuple-element.19.w11_ref, f32[128,128]{1,0:T(8,128)S(1)} %get-tuple-element.20.l_ref, f32[128,128]{1,0:T(8,128)S(1)} %get-tuple-element.21.s_ref, f32[1024,256]{1,0:T(8,128)S(1)} %get-tuple-element.22.p_ref), custom_call_target="tpu_custom_call" | custom-call | tf_op jit(solution)/shard_map/factor_last/pallas_call | solution.py:276
  119.5 0.0 copy-start
  119.5 0.7 copy-done
  120.2 0.0 all-to-all-done.3
  120.2 0.0 copy-start.1
  120.2 0.9 copy-done.1
  121.2 11.0 %update.1 = (f32[10,1024,128]{2,1,0:T(8,128)}, f32[10,256,128]{2,1,0:T(8,128)}) custom-call(f32[256,256]{1,0:T(8,128)S(1)} %copy-done.1, f32[256,1280]{1,0:T(8,128)S(1)} %bitcast.17, f32[1024,256]{1,0:T(8,128)S(1)} %get-tuple-element.25.q_ref, f32[10,1024,128]{2,1,0:T(8,128)} %bitcast.22), custom_call_target="tpu_custom_call" | custom-call | tf_op jit(solution)/shard_map/update/pallas_call | solution.py:299
  (7 shorter events, 0.0 us)
Async XLA Ops:
  1.7 11.4 %collective-permute-start.4 = (f32[512,128]{1,0:T(8,128)S(1)}, f32[512,128]{1,0:T(8,128)S(1)}, u32[]{:S(2)}, u32[]{:S(2)}) collective-permute-start(f32[512,128]{1,0:T(8,128)S(1)} %get-tuple-element.30), channel_id=1, source_target_pairs={{0,6},{1,7},{8,14},{9,15},{16,22},{17,23},{24,30},{25,31},{32,38},... | collective-permute-start | bytes 786440 | tf_op jit(solution)/shard_map/ppermute | solution.py:36
  6.4 8.0 %collective-permute-start = (f32[512,128]{1,0:T(8,128)S(1)}, f32[512,128]{1,0:T(8,128)S(1)}, u32[]{:S(2)}, u32[]{:S(2)}) collective-permute-start(f32[512,128]{1,0:T(8,128)S(1)} %get-tuple-element.31), channel_id=1, source_target_pairs={{0,2},{1,3},{8,10},{9,11},{16,18},{17,19},{24,26},{25,27},{32,34},... | collective-permute-start | bytes 786440 | tf_op jit(solution)/shard_map/ppermute | solution.py:35
  7.7 11.1 %collective-permute-start.3 = (f32[512,128]{1,0:T(8,128)S(1)}, f32[512,128]{1,0:T(8,128)S(1)}, u32[]{:S(2)}, u32[]{:S(2)}) collective-permute-start(f32[512,128]{1,0:T(8,128)S(1)} %get-tuple-element.30), channel_id=1, source_target_pairs={{0,2},{1,3},{8,10},{9,11},{16,18},{17,19},{24,26},{25,27},{32,34},... | collective-permute-start | bytes 786440 | tf_op jit(solution)/shard_map/ppermute | solution.py:37
  9.0 9.8 %collective-permute-start.2 = (f32[512,128]{1,0:T(8,128)S(1)}, f32[512,128]{1,0:T(8,128)S(1)}, u32[]{:S(2)}, u32[]{:S(2)}) collective-permute-start(f32[512,128]{1,0:T(8,128)S(1)} %get-tuple-element.31), channel_id=1, source_target_pairs={{0,6},{1,7},{8,14},{9,15},{16,22},{17,23},{24,30},{25,31},{32,38},... | collective-permute-start | bytes 786440 | tf_op jit(solution)/shard_map/ppermute | solution.py:38
  13.1 5.8 %collective-permute-start.5 = (f32[512,128]{1,0:T(8,128)S(1)}, f32[512,128]{1,0:T(8,128)S(1)}, u32[]{:S(2)}, u32[]{:S(2)}) collective-permute-start(f32[512,128]{1,0:T(8,128)S(1)} %collective-permute-done.4), channel_id=1, source_target_pairs={{6,4},{7,5},{14,12},{15,13},{22,20},{23,21},{30,28},{31,29},{38,36... | collective-permute-start | bytes 786440 | tf_op jit(solution)/shard_map/ppermute | solution.py:40
  14.4 4.5 %collective-permute-start.1 = (f32[512,128]{1,0:T(8,128)S(1)}, f32[512,128]{1,0:T(8,128)S(1)}, u32[]{:S(2)}, u32[]{:S(2)}) collective-permute-start(f32[512,128]{1,0:T(8,128)S(1)} %collective-permute-done), channel_id=1, source_target_pairs={{2,4},{3,5},{10,12},{11,13},{18,20},{19,21},{26,28},{27,29},{34,36... | collective-permute-start | bytes 786440 | tf_op jit(solution)/shard_map/ppermute | solution.py:39
  20.0 1.6 %collective-permute-start.7 = (f32[512,128]{1,0:T(8,128)S(1)}, f32[512,128]{1,0:T(8,128)S(1)}, u32[]{:S(2)}, u32[]{:S(2)}) collective-permute-start(f32[512,128]{1,0:T(8,128)S(1)} %get-tuple-element.28.mh_ref), channel_id=1, source_target_pairs={{0,1},{1,0},{2,3},{3,2},{4,5},{5,4},{6,7},{7,6},{8,9},{9,8},{10,11... | collective-permute-start | bytes 786440 | tf_op jit(solution)/shard_map/ppermute | solution.py:28
  20.1 1.9 %collective-permute-start.6 = (f32[512,128]{1,0:T(8,128)S(1)}, f32[512,128]{1,0:T(8,128)S(1)}, u32[]{:S(2)}, u32[]{:S(2)}) collective-permute-start(f32[512,128]{1,0:T(8,128)S(1)} %get-tuple-element.29.ml_ref), channel_id=1, source_target_pairs={{0,1},{1,0},{2,3},{3,2},{4,5},{5,4},{6,7},{7,6},{8,9},{9,8},{10,11... | collective-permute-start | bytes 786440 | tf_op jit(solution)/shard_map/ppermute | solution.py:28
  75.5 11.8 %collective-permute-start.10 = (f32[8,256]{1,0:T(8,128)S(1)}, f32[8,256]{1,0:T(8,128)S(1)}, u32[]{:S(2)}, u32[]{:S(2)}) collective-permute-start(f32[8,256]{1,0:T(8,128)S(1)} %get-tuple-element.17), channel_id=1, source_target_pairs={{0,2},{2,4},{4,6},{6,0},{1,3},{3,5},{5,7},{7,1},{8,10},{10,12},{12... | collective-permute-start | bytes 24584 | tf_op jit(solution)/shard_map/ppermute | solution.py:155
  78.7 8.6 %collective-permute-start.9 = (f32[8,256]{1,0:T(8,128)S(1)}, f32[8,256]{1,0:T(8,128)S(1)}, u32[]{:S(2)}, u32[]{:S(2)}) collective-permute-start(f32[8,256]{1,0:T(8,128)S(1)} %get-tuple-element.17), channel_id=1, source_target_pairs={{0,4},{2,6},{4,0},{6,2},{1,5},{3,7},{5,1},{7,3},{8,12},{10,14},{12... | collective-permute-start | bytes 24584 | tf_op jit(solution)/shard_map/ppermute | solution.py:155
  81.2 6.1 %collective-permute-start.8 = (f32[8,256]{1,0:T(8,128)S(1)}, f32[8,256]{1,0:T(8,128)S(1)}, u32[]{:S(2)}, u32[]{:S(2)}) collective-permute-start(f32[8,256]{1,0:T(8,128)S(1)} %get-tuple-element.17), channel_id=1, source_target_pairs={{0,6},{2,0},{4,2},{6,4},{1,7},{3,1},{5,3},{7,5},{8,14},{10,8},{12,... | collective-permute-start | bytes 24584 | tf_op jit(solution)/shard_map/ppermute | solution.py:155
  83.8 14.5 %all-to-all-start.2 = ((f32[8,8,1280]{2,1,0:T(8,128)}), f32[8,8,1280]{2,1,0:T(8,128)S(1)}, u32[]{:S(2)}, u32[]{:S(2)}) async-start(f32[8,8,1280]{2,1,0:T(8,128)} %get-tuple-element.16), calls=%async_computation.2 | async-start | bytes 655360 | tf_op jit(solution)/shard_map/all_to_all | solution.py:322
  87.4 4.8 %collective-permute-start.11 = (f32[32,256]{1,0:T(8,128)S(1)}, f32[32,256]{1,0:T(8,128)S(1)}, u32[]{:S(2)}, u32[]{:S(2)}) collective-permute-start(f32[32,256]{1,0:T(8,128)S(1)} %get-tuple-element.32), channel_id=1, source_target_pairs={{0,24},{8,0},{16,8},{24,16},{1,25},{9,1},{17,9},{25,17},{2,26},{10... | collective-permute-start | bytes 98312 | tf_op jit(solution)/shard_map/ppermute | solution.py:155
  88.9 6.0 %collective-permute-start.13 = (f32[32,256]{1,0:T(8,128)S(1)}, f32[32,256]{1,0:T(8,128)S(1)}, u32[]{:S(2)}, u32[]{:S(2)}) collective-permute-start(f32[32,256]{1,0:T(8,128)S(1)} %get-tuple-element.32), channel_id=1, source_target_pairs={{0,8},{8,16},{16,24},{24,0},{1,9},{9,17},{17,25},{25,1},{2,10},{10... | collective-permute-start | bytes 98312 | tf_op jit(solution)/shard_map/ppermute | solution.py:155
  89.5 5.4 %collective-permute-start.12 = (f32[32,256]{1,0:T(8,128)S(1)}, f32[32,256]{1,0:T(8,128)S(1)}, u32[]{:S(2)}, u32[]{:S(2)}) collective-permute-start(f32[32,256]{1,0:T(8,128)S(1)} %get-tuple-element.32), channel_id=1, source_target_pairs={{0,16},{8,24},{16,0},{24,8},{1,17},{9,25},{17,1},{25,9},{2,18},{10... | collective-permute-start | bytes 98312 | tf_op jit(solution)/shard_map/ppermute | solution.py:155
  99.5 20.7 %all-to-all-start.3 = ((f32[4,64,1280]{2,1,0:T(8,128)}), f32[4,64,1280]{2,1,0:T(8,128)S(1)}, u32[]{:S(2)}, u32[]{:S(2)}) async-start(f32[4,64,1280]{2,1,0:T(8,128)} %broadcast_in_dim.20), calls=%async_computation.3 | async-start | bytes 2621440 | tf_op jit(solution)/shard_map/all_to_all | solution.py:322
  104.5 1.3 %collective-permute-start.14 = (f32[128,256]{1,0:T(8,128)S(1)}, f32[128,256]{1,0:T(8,128)S(1)}, u32[]{:S(2)}, u32[]{:S(2)}) collective-permute-start(f32[128,256]{1,0:T(8,128)S(1)} %constant_dynamic-update-slice_fusion.4.mine_ref), channel_id=1, source_target_pairs={{0,1},{1,0},{2,3},{3,2},{4,5},{5,4},{6,7},{7,6},{8,9},{9,8},{10,11... | collective-permute-start | bytes 393224 | tf_op jit(solution)/shard_map/ppermute | solution.py:28
  119.5 0.7 copy-start
  120.2 1.0 copy-start.1

commit v5 on v4

--- a/solution.py
+++ b/solution.py
@@ -10,11 +10,39 @@
 LANES, SUB = 128, 8
 RIDE = 1280
 NT = (((1,), (1,)), ((), ()))
-PARAMS = pltpu.CompilerParams(vmem_limit_bytes=48 << 20)
+VMEM = pl.BlockSpec(memory_space=pltpu.VMEM)
+HBM = pl.BlockSpec(memory_space=pltpu.HBM)
+
+
+def in_hbm(values):
+    return pltpu.with_memory_space_constraint(values, pltpu.HBM)
+
+
+def params(mib):
+    return pltpu.CompilerParams(vmem_limit_bytes=mib << 20)
 
 
 def dot(left, right, dims=(((1,), (0,)), ((), ()))):
     return lax.dot_general(left, right, dims, precision=PRECISE, preferred_element_type=jnp.float32)
+
+
+def split(values):
+    high = values.astype(jnp.bfloat16)
+    return high, (values - high.astype(jnp.float32)).astype(jnp.bfloat16)
+
+
+def wide_left(values):
+    high, low = split(values)
+    return jnp.concatenate([high, high, low], axis=1)
+
+
+def wide_right(values):
+    high, low = split(values)
+    return jnp.concatenate([high, low, high], axis=0)
+
+
+def narrow_dot(left, right):
+    return lax.dot_general(left, right, (((1,), (0,)), ((), ())), preferred_element_type=jnp.float32)
 
 
 def pick(index, choices):
@@ -50,10 +78,6 @@
 SCALAR = pl.BlockSpec(memory_space=pltpu.SMEM)
 
 
-def whole(shape):
-    return pl.BlockSpec(shape, lambda i: (0,) * len(shape))
-
-
 def place(core, pieces, p_ref):
     half, k = pieces[0].shape
     first = core == 0
@@ -64,27 +88,39 @@
         p_ref[rows, k:] = jnp.where(first, other, mine)
 
 
-def products_kernel(x_ref, core_ref, ml_ref, mh_ref, ol_ref, oh_ref, c_ref, o_ref, p_ref, pt_ref):
-    i = pl.program_id(0)
-    k = c_ref.shape[2]
+def fetch(source, target, sem):
+    copies = [pltpu.make_async_copy(source.at[r], target.at[r], sem.at[r]) for r in range(source.shape[0])]
+    for copy in copies:
+        copy.start()
+    return copies
+
+
+def products_kernel(x_ref, core_ref, ml_ref, mh_ref, ol_ref, oh_ref, c_hbm, o_ref, p_hbm, c_ref, p_ref, t_ref, sem, p_sem):
+    rounds, n, k = c_ref.shape
     w = 2 * k
-
-    @pl.when(i == 0)
-    def _():
-        place(core_ref[0], (ml_ref, mh_ref, ol_ref, oh_ref), p_ref)
-        pt_ref[...] = p_ref[...].T
-        share = NY * SUB
-        at = pl.multiple_of((x_ref[0] * NC + core_ref[0]) * share, share)
-        gram = dot(pt_ref[pl.ds(at, share), :], p_ref[...])
-        o_ref[:, RIDE:] = jnp.zeros((w, LANES), jnp.float32)
-        for y in range(NY):
-            row = y * (w // NY)
-            piece = gram[y * SUB : (y + 1) * SUB]
-            o_ref[row : row + SUB, RIDE:] = piece[:, :LANES]
-            o_ref[row + SUB : row + 2 * SUB, RIDE:] = piece[:, LANES:]
-
-    lanes = pl.ds(pl.multiple_of(i * w, w), w)
-    o_ref[:, lanes] = dot(pt_ref[...], jnp.concatenate([c_ref[0], c_ref[1]], axis=1))
+    arriving = fetch(c_hbm, c_ref, sem)
+    place(core_ref[0], (ml_ref, mh_ref, ol_ref, oh_ref), p_ref)
+    leaving = pltpu.make_async_copy(p_ref, p_hbm, p_sem)
+    leaving.start()
+    turned = p_ref[...].T
+    t_ref[...] = turned
+    left = wide_left(turned)
+    share = NY * SUB
+    at = pl.multiple_of((x_ref[0] * NC + core_ref[0]) * share, share)
+    gram = dot(t_ref[pl.ds(at, share), :], p_ref[...])
+    o_ref[:, RIDE:] = jnp.zeros((w, LANES), jnp.float32)
+    for y in range(NY):
+        row = y * (w // NY)
+        piece = gram[y * SUB : (y + 1) * SUB]
+        o_ref[row : row + SUB, RIDE:] = piece[:, :LANES]
+        o_ref[row + SUB : row + 2 * SUB, RIDE:] = piece[:, LANES:]
+    group = rounds // 2
+    for r in range(0, rounds, group):
+        for copy in arriving[r : r + group]:
+            copy.wait()
+        some = jnp.concatenate([c_ref[at] for at in range(r, r + group)], axis=1)
+        o_ref[:, r * k : (r + group) * k] = narrow_dot(left, wide_right(some))
+    leaving.wait()
 
 
 def products(pieces, columns):
@@ -92,17 +128,20 @@
     w = 2 * k
     return pl.pallas_call(
         products_kernel,
-        grid=(rounds // 2,),
-        in_specs=[SCALAR, SCALAR]
-        + [whole((n // 2, k))] * 4
-        + [pl.BlockSpec((2, n, k), lambda i: (i, 0, 0))],
-        out_specs=[whole((w, RIDE + LANES)), whole((n, w))],
+        in_specs=[SCALAR, SCALAR] + [VMEM] * 4 + [HBM],
+        out_specs=[VMEM, HBM],
         out_shape=[
             jax.ShapeDtypeStruct((w, RIDE + LANES), jnp.float32),
             jax.ShapeDtypeStruct((n, w), jnp.float32),
         ],
-        scratch_shapes=[pltpu.VMEM((w, n), jnp.float32)],
-        compiler_params=PARAMS,
+        scratch_shapes=[
+            pltpu.VMEM(columns.shape, jnp.float32),
+            pltpu.VMEM((n, w), jnp.float32),
+            pltpu.VMEM((w, n), jnp.float32),
+            pltpu.SemaphoreType.DMA((rounds,)),
+            pltpu.SemaphoreType.DMA(()),
+        ],
+        compiler_params=params(20),
         name="products",
     )(index_of("x"), index_of("c"), *pieces, columns)
 
@@ -119,34 +158,43 @@
     out = (NZ, SUB, RIDE + 2 * LANES)
     return pl.pallas_call(
         sum_y_kernel,
-        grid=(1,),
-        in_specs=[whole(pieces.shape)],
-        out_specs=whole(out),
+        in_specs=[VMEM],
+        out_specs=VMEM,
         out_shape=jax.ShapeDtypeStruct(out, jnp.float32),
-        compiler_params=PARAMS,
+        compiler_params=params(8),
         name="sum_y",
     )(pieces)
 
 
-def sum_z_kernel(a_ref, o_ref, g_ref):
-    total = a_ref[0]
+def total_z(a_ref, lanes):
+    total = a_ref[0, :, lanes]
     for z in range(1, NZ):
-        total = total + a_ref[z]
+        total = total + a_ref[z, :, lanes]
+    return total
+
+
+def copies_z_kernel(a_ref, o_ref):
+    total = total_z(a_ref, slice(0, RIDE))
     for z in range(NZ):
-        o_ref[z] = total[:, :RIDE]
-    g_ref[...] = total[:, RIDE:]
-
-
-def sum_z(pieces):
-    copies, gram = (NZ, SUB, RIDE), (SUB, 2 * LANES)
-    return pl.pallas_call(
-        sum_z_kernel,
-        grid=(1,),
-        in_specs=[whole(pieces.shape)],
-        out_specs=[whole(copies), whole(gram)],
-        out_shape=[jax.ShapeDtypeStruct(copies, jnp.float32), jax.ShapeDtypeStruct(gram, jnp.float32)],
-        compiler_params=PARAMS,
-        name="sum_z",
+        o_ref[z] = total
+
+
+def gram_z_kernel(a_ref, o_ref):
+    o_ref[...] = total_z(a_ref, slice(RIDE, RIDE + 2 * LANES))
+
+
+LATE = pl.CostEstimate(flops=10**10, transcendentals=0, bytes_accessed=10**8)
+
+
+def sum_z(pieces, kernel, out, name, cost=None):
+    return pl.pallas_call(
+        kernel,
+        in_specs=[VMEM],
+        out_specs=VMEM,
+        out_shape=jax.ShapeDtypeStruct(out, jnp.float32),
+        cost_estimate=cost,
+        compiler_params=params(8),
+        name=name,
     )(pieces)
 
 
@@ -246,76 +294,93 @@
     s_ref[...] = g_ref[h:, h:] - dot(l21, l21, NT)
 
 
-def factor_last_kernel(w11_ref, l_ref, s_ref, p_ref, w_ref, q_ref):
+def factor_last_kernel(w11_ref, l_ref, s_ref, p_hbm, w_ref, q_ref, p_ref, sem):
+    arriving = pltpu.make_async_copy(p_hbm, p_ref, sem)
+    arriving.start()
     h = LANES
     w11 = w11_ref[...]
     w_ref[:h, :h] = w11
     w_ref[:h, h:] = jnp.zeros((h, h), jnp.float32)
     invert_factor(s_ref[...], w_ref, h, h)
     w_ref[h:, :h] = -dot(w_ref[h:, h:], dot(l_ref[...], w11))
-    q_ref[...] = dot(p_ref[...], w_ref[...], NT)
+    arriving.wait()
+    q_ref[...] = wide_left(dot(p_ref[...], w_ref[...], NT))
 
 
 def factor_first(mine, other):
     h, w = mine.shape
     return pl.pallas_call(
         factor_first_kernel,
-        grid=(1,),
-        in_specs=[SCALAR] * 3 + [whole((h, w))] * 2,
-        out_specs=[whole((h, h))] * 3,
+        in_specs=[SCALAR] * 3 + [VMEM] * 2,
+        out_specs=[VMEM] * 3,
         out_shape=[jax.ShapeDtypeStruct((h, h), jnp.float32)] * 3,
         scratch_shapes=[pltpu.VMEM((w, w), jnp.float32)],
-        compiler_params=PARAMS,
+        compiler_params=params(8),
         name="factor_first",
     )(index_of("x"), index_of("y"), index_of("c"), mine, other)
 
 
 def factor_last(w11, l21, schur, panels):
     n, w = panels.shape
-    h = w // 2
     return pl.pallas_call(
         factor_last_kernel,
-        grid=(1,),
-        in_specs=[whole((h, h))] * 3 + [whole((n, w))],
-        out_specs=[whole((w, w)), whole((n, w))],
-        out_shape=[jax.ShapeDtypeStruct((w, w), jnp.float32), jax.ShapeDtypeStruct((n, w), jnp.float32)],
-        compiler_params=PARAMS,
+        in_specs=[VMEM] * 3 + [HBM],
+        out_specs=[VMEM] * 2,
+        out_shape=[jax.ShapeDtypeStruct((w, w), jnp.float32), jax.ShapeDtypeStruct((n, 3 * w), jnp.bfloat16)],
+        scratch_shapes=[pltpu.VMEM((n, w), jnp.float32), pltpu.SemaphoreType.DMA(())],
+        compiler_params=params(12),
         name="factor_last",
     )(w11, l21, schur, panels)
 
 
-def update_kernel(w_ref, x_ref, q_ref, c_ref, red_ref, top_ref):
-    k = c_ref.shape[2]
-    top = dot(w_ref[...], x_ref[...])
-    fit = dot(q_ref[...], top)
-    for at in range(2):
-        top_ref[at] = top[:, at * k : (at + 1) * k]
-        red_ref[at] = c_ref[at] - fit[:, at * k : (at + 1) * k]
+BAND = 256
+
+
+def update_kernel(w_ref, q_ref, x_ref, c_hbm, red_hbm, top_hbm, red_ref, top_ref, c_sem, red_sem, top_sem):
+    rounds, n, k = red_ref.shape
+    bands = [pl.ds(at, BAND) for at in range(0, n, BAND)]
+    arriving = [
+        pltpu.make_async_copy(c_hbm.at[:, band], red_ref.at[:, band], c_sem.at[at]) for at, band in enumerate(bands)
+    ]
+    for copy in arriving:
+        copy.start()
+    top = narrow_dot(wide_left(w_ref[...]), wide_right(x_ref[...]))
+    for r in range(rounds):
+        top_ref[r] = top[:, r * k : (r + 1) * k]
+    leaving = [pltpu.make_async_copy(top_ref, top_hbm, top_sem)]
+    leaving[0].start()
+    right = wide_right(top)
+    for at, band in enumerate(bands):
+        fit = narrow_dot(q_ref[at * BAND : (at + 1) * BAND], right)
+        arriving[at].wait()
+        for r in range(rounds):
+            red_ref[r, at * BAND : (at + 1) * BAND] -= fit[:, r * k : (r + 1) * k]
+        copy = pltpu.make_async_copy(red_ref.at[:, band], red_hbm.at[:, band], red_sem.at[at])
+        copy.start()
+        leaving.append(copy)
+    for copy in leaving:
+        copy.wait()
 
 
 def update(inverse, basis, cross, columns):
     rounds, n, k = columns.shape
     w = inverse.shape[0]
+    reduced, top = (rounds, n, k), (rounds, w, k)
     return pl.pallas_call(
         update_kernel,
-        grid=(rounds // 2,),
-        in_specs=[
-            pl.BlockSpec((w, w), lambda i: (0, 0)),
-            pl.BlockSpec((w, 2 * k), lambda i: (0, i)),
-            pl.BlockSpec((n, w), lambda i: (0, 0)),
-            pl.BlockSpec((2, n, k), lambda i: (i, 0, 0)),
+        in_specs=[VMEM] * 3 + [HBM],
+        out_specs=[HBM] * 2,
+        out_shape=[jax.ShapeDtypeStruct(reduced, jnp.float32), jax.ShapeDtypeStruct(top, jnp.float32)],
+        scratch_shapes=[
+            pltpu.VMEM(reduced, jnp.float32),
+            pltpu.VMEM(top, jnp.float32),
+            pltpu.SemaphoreType.DMA((n // BAND,)),
+            pltpu.SemaphoreType.DMA((n // BAND,)),
+            pltpu.SemaphoreType.DMA(()),
         ],
-        out_specs=[
-            pl.BlockSpec((2, n, k), lambda i: (i, 0, 0)),
-            pl.BlockSpec((2, w, k), lambda i: (i, 0, 0)),
-        ],
-        out_shape=[
-            jax.ShapeDtypeStruct((rounds, n, k), jnp.float32),
-            jax.ShapeDtypeStruct((rounds, w, k), jnp.float32),
-        ],
-        compiler_params=PARAMS,
+        compiler_params=params(24),
         name="update",
-    )(inverse, cross, basis, columns)
+    )(inverse, basis, cross, columns)
 
 
 def exchange(pieces, axis):
@@ -325,14 +390,18 @@
 def shards(matrix):
     hold = lax.optimization_barrier
     columns = jnp.transpose(matrix, (1, 0, 2))
-    both, panels = products(relay(columns[0]), columns)
+    own, columns = columns[0], in_hbm(columns)
+    both, panels = products(relay(own), columns)
     w = panels.shape[1]
     pieces = sum_y(exchange(both.reshape(NY, w // NY, RIDE + LANES), "y"))
-    copies, gram = sum_z(exchange(pieces, "z"))
+    pieces = exchange(pieces, "z")
+    copies = sum_z(pieces, copies_z_kernel, (NZ, SUB, RIDE), "copies_z")
+    copies, pieces = hold((copies, pieces))
+    gram = sum_z(pieces, gram_z_kernel, (SUB, 2 * LANES), "gram_z", LATE)
     part = exchange(copies, "z").reshape(w // NY, RIDE)
     gram = collect(collect(gram, "x", NX), "y", NY)
     part, gram = hold((part, gram))
-    inverse, basis = factor_last(*factor_first(gram, swap(gram)), panels)
+    inverse, basis = factor_last(*factor_first(gram, swap(gram)), in_hbm(panels))
     cross = exchange(jnp.broadcast_to(part[None], (NY, w // NY, RIDE)), "y").reshape(w, RIDE)
     reduced, top = update(inverse, basis, cross, columns)
     return jnp.transpose(reduced, (1, 0, 2)), jnp.transpose(top, (1, 0, 2))

time: 134 us -> 124 us (0.925)
  Pallas kernels: 33.5 us -> 25.6 us
  local copies, waits for them, and re-layouts: 3.9 us -> 2.25 us
    pallas_call x6 -> x7, Pallas kernels: 33.5 us -> 25.6 us  [the longest x1 7.75 us: factor_last(): pl.pallas_call(factor_last_kernel, in_specs=[VMEM] * 3 + [HBM], out_specs...]
    unnamed x9 -> x8, local copies, waits for them, and re-layouts: 1.67 us -> 0.02 us
  transfers between devices with their start and end apart: 17 -> 17, of which waited for: 8 -> 8; matrix products, arithmetic and copies ran while one was open for 0% -> 0% of each run, Pallas kernels for 10% -> 12%
where the time goes in v5:
time: 124 us; the launch traced here: 123 us
  blocking collectives  44.7 us (36%)
  starting transfers between devices  31.5 us (25%)
  Pallas kernels  25.6 us (21%)
  waiting for transfers between devices  16.8 us (14%)
  local copies, waits for them, and re-layouts  2.25 us (2%)
    all_to_all x2, blocking collectives, exchange(): return lax.all_to_all(pieces, axis, 0, 0)  44.7 us
    ppermute x6, starting transfers between devices, collect(): lax.ppermute(values, axis, pairs)  12.6 us
    all_to_all x2, starting transfers between devices, exchange(): return lax.all_to_all(pieces, axis, 0, 0)  8.4 us
    pallas_call x1, Pallas kernels, factor_last(): pl.pallas_call(factor_last_kernel, in_specs=[VMEM] * 3 + [HBM], out_specs...  7.75 us
    pallas_call x1, Pallas kernels, factor_first(): pl.pallas_call(factor_first_kernel, in_specs=[SCALAR] * 3 + [VMEM] * 2, o...  6.59 us
    pallas_call x1, Pallas kernels, update(): pl.pallas_call(update_kernel, in_specs=[VMEM] * 3 + [HBM], out_specs=[HBM...  5.43 us
    pallas_call x1, Pallas kernels, products(): pl.pallas_call(products_kernel, in_specs=[SCALAR, SCALAR] + [VMEM] * 4 +...  4.97 us
    ppermute x1, starting transfers between devices, relay(): down_high = lax.ppermute(high, 'x', [(0, 3)])  4.68 us
  transfers between devices with their start and end apart: 17, of which 8 were waited for; matrix products, arithmetic and copies ran while one was open for 0% of the time, Pallas kernels for 12%

profile of v5, /device:TPU:8, one launch (start us, length us, event | category | flops | bytes accessed | tf_op | source)
XLA Modules:
  0.0 122.8 jit_solution(9364622058370096170)
XLA Ops:
  0.6 1.1 slice_bitcast_fusion
  1.7 4.7 %collective-permute-start.4 = (f32[512,128]{1,0:T(8,128)S(1)}, f32[512,128]{1,0:T(8,128)S(1)}, u32[]{:S(2)}, u32[]{:S(2)}) collective-permute-start(f32[512,128]{1,0:T(8,128)S(1)} %get-tuple-element.30), channel_id=1, source_target_pairs={{0,6},{1,7},{8,14},{9,15},{16,22},{17,23},{24,30},{25,31},{32,38},... | collective-permute-start | bytes 786440 | tf_op jit(solution)/shard_map/ppermute | solution.py:64
  6.4 1.3 %collective-permute-start = (f32[512,128]{1,0:T(8,128)S(1)}, f32[512,128]{1,0:T(8,128)S(1)}, u32[]{:S(2)}, u32[]{:S(2)}) collective-permute-start(f32[512,128]{1,0:T(8,128)S(1)} %get-tuple-element.31), channel_id=1, source_target_pairs={{0,2},{1,3},{8,10},{9,11},{16,18},{17,19},{24,26},{25,27},{32,34},... | collective-permute-start | bytes 786440 | tf_op jit(solution)/shard_map/ppermute | solution.py:63
  7.7 1.3 %collective-permute-start.3 = (f32[512,128]{1,0:T(8,128)S(1)}, f32[512,128]{1,0:T(8,128)S(1)}, u32[]{:S(2)}, u32[]{:S(2)}) collective-permute-start(f32[512,128]{1,0:T(8,128)S(1)} %get-tuple-element.30), channel_id=1, source_target_pairs={{0,2},{1,3},{8,10},{9,11},{16,18},{17,19},{24,26},{25,27},{32,34},... | collective-permute-start | bytes 786440 | tf_op jit(solution)/shard_map/ppermute | solution.py:65
  9.0 1.3 %collective-permute-start.2 = (f32[512,128]{1,0:T(8,128)S(1)}, f32[512,128]{1,0:T(8,128)S(1)}, u32[]{:S(2)}, u32[]{:S(2)}) collective-permute-start(f32[512,128]{1,0:T(8,128)S(1)} %get-tuple-element.31), channel_id=1, source_target_pairs={{0,6},{1,7},{8,14},{9,15},{16,22},{17,23},{24,30},{25,31},{32,38},... | collective-permute-start | bytes 786440 | tf_op jit(solution)/shard_map/ppermute | solution.py:66
  10.3 2.7 %collective-permute-done.4 = f32[512,128]{1,0:T(8,128)S(1)} collective-permute-done((f32[512,128]{1,0:T(8,128)S(1)}, f32[512,128]{1,0:T(8,128)S(1)}, u32[]{:S(2)}, u32[]{:S(2)}) %collective-permute-start.4) | collective-permute-done | bytes 262176 | tf_op jit(solution)/shard_map/ppermute | solution.py:64
  13.1 0.7 collective-permute-start.5
  13.7 0.6 collective-permute-done
  14.4 0.7 collective-permute-start.1
  15.1 3.8 %collective-permute-done.3 = f32[512,128]{1,0:T(8,128)S(1)} collective-permute-done((f32[512,128]{1,0:T(8,128)S(1)}, f32[512,128]{1,0:T(8,128)S(1)}, u32[]{:S(2)}, u32[]{:S(2)}) %collective-permute-start.3) | collective-permute-done | bytes 262176 | tf_op jit(solution)/shard_map/ppermute | solution.py:65
  18.8 0.0 collective-permute-done.2
  18.9 0.0 collective-permute-done.5
  18.9 0.0 collective-permute-done.1
  18.9 1.1 select_select_fusion
  20.0 0.1 collective-permute-start.7
  20.1 0.5 collective-permute-start.6
  20.6 1.0 collective-permute-done.7.oh_ref
  21.6 0.4 collective-permute-done.6.ol_ref
  22.0 5.0 %products.1 = (f32[256,1408]{1,0:T(8,128)S(1)}, f32[1024,256]{1,0:T(8,128)S(1)}) custom-call(s32[1]{0:T(128)} %bitcast.x_ref, s32[1]{0:T(128)} %bitcast.2.core_ref, f32[512,128]{1,0:T(8,128)S(1)} %get-tuple-element.29.ml_ref, f32[512,128]{1,0:T(8,128)S(1)} %get-tuple-element.28.mh_ref, f32[512,128]{1,0:T(8,128)S(1)} %collective-permute-done.6.ol_ref, ...), custom_call_target="tpu_custom_call" | custom-call | tf_op jit(solution)/shard_map/products/pallas_call | solution.py:129
  27.0 0.0 copy-start
  27.0 22.9 %all_to_all.20.a_ref = f32[4,64,1408]{2,1,0:T(8,128)S(1)} all-to-all(f32[4,64,1408]{2,1,0:T(8,128)S(1)} %bitcast.18), channel_id=1, replica_groups=mesh['z'=8,'y'=4,'x'=4,'c'=2] {'y'}, dimensions={0} | all-to-all | bytes 2883584 | tf_op jit(solution)/shard_map/all_to_all | solution.py:387
  49.8 0.1 sum_y.1
  49.9 0.0 copy-done
  49.9 21.8 %all_to_all.21.a_ref = f32[8,8,1536]{2,1,0:T(8,128)S(1)} all-to-all(f32[8,8,1536]{2,1,0:T(8,128)S(1)} %sum_y.1), channel_id=1, replica_groups=mesh['z'=8,'y'=4,'x'=4,'c'=2] {'z'}, dimensions={0} | all-to-all | bytes 786432 | tf_op jit(solution)/shard_map/all_to_all | solution.py:387
  71.7 0.8 copies_z.1
  72.5 3.2 %collective-permute-start.10 = (f32[8,256]{1,0:T(8,128)S(1)}, f32[8,256]{1,0:T(8,128)S(1)}, u32[]{:S(2)}, u32[]{:S(2)}) collective-permute-start(f32[8,256]{1,0:T(8,128)S(1)} %gram_z.1), channel_id=1, source_target_pairs={{0,2},{2,4},{4,6},{6,0},{1,3},{3,5},{5,7},{7,1},{8,10},{10,12},{12... | collective-permute-start | bytes 24584 | tf_op jit(solution)/shard_map/ppermute | solution.py:203
  75.7 2.6 %collective-permute-start.9 = (f32[8,256]{1,0:T(8,128)S(1)}, f32[8,256]{1,0:T(8,128)S(1)}, u32[]{:S(2)}, u32[]{:S(2)}) collective-permute-start(f32[8,256]{1,0:T(8,128)S(1)} %gram_z.1), channel_id=1, source_target_pairs={{0,4},{2,6},{4,0},{6,2},{1,5},{3,7},{5,1},{7,3},{8,12},{10,14},{12... | collective-permute-start | bytes 24584 | tf_op jit(solution)/shard_map/ppermute | solution.py:203
  78.3 2.5 %collective-permute-start.8 = (f32[8,256]{1,0:T(8,128)S(1)}, f32[8,256]{1,0:T(8,128)S(1)}, u32[]{:S(2)}, u32[]{:S(2)}) collective-permute-start(f32[8,256]{1,0:T(8,128)S(1)} %gram_z.1), channel_id=1, source_target_pairs={{0,6},{2,0},{4,2},{6,4},{1,7},{3,1},{5,3},{7,5},{8,14},{10,8},{12,... | collective-permute-start | bytes 24584 | tf_op jit(solution)/shard_map/ppermute | solution.py:203
  80.9 3.4 %all-to-all-start.2 = ((f32[8,8,1280]{2,1,0:T(8,128)}), f32[8,8,1280]{2,1,0:T(8,128)S(1)}, u32[]{:S(2)}, u32[]{:S(2)}) async-start(f32[8,8,1280]{2,1,0:T(8,128)} %copies_z.1), calls=%async_computation.2 | async-start | bytes 655360 | tf_op jit(solution)/shard_map/all_to_all | solution.py:387
  84.3 0.0 collective-permute-done.10
  84.3 0.0 collective-permute-done.9
  84.3 0.0 collective-permute-done.8
  84.4 0.4 collective-permute-start.13
  84.7 3.2 %collective-permute-start.12 = (f32[32,256]{1,0:T(8,128)S(1)}, f32[32,256]{1,0:T(8,128)S(1)}, u32[]{:S(2)}, u32[]{:S(2)}) collective-permute-start(f32[32,256]{1,0:T(8,128)S(1)} %pad_maximum_fusion), channel_id=1, source_target_pairs={{0,16},{8,24},{16,0},{24,8},{1,17},{9,25},{17,1},{25,9},{2,18},{10... | collective-permute-start | bytes 98312 | tf_op jit(solution)/shard_map/ppermute | solution.py:203
  88.0 0.6 collective-permute-start.11
  88.5 3.3 %collective-permute-done.11 = f32[32,256]{1,0:T(8,128)S(1)} collective-permute-done((f32[32,256]{1,0:T(8,128)S(1)}, f32[32,256]{1,0:T(8,128)S(1)}, u32[]{:S(2)}, u32[]{:S(2)}) %collective-permute-start.11) | collective-permute-done | bytes 32800 | tf_op jit(solution)/shard_map/ppermute | solution.py:203
  91.9 0.0 collective-permute-done.12
  91.9 0.0 collective-permute-done.13
  91.9 3.5 %all-to-all-done.2 = f32[8,8,1280]{2,1,0:T(8,128)S(1)} async-done(((f32[8,8,1280]{2,1,0:T(8,128)}), f32[8,8,1280]{2,1,0:T(8,128)S(1)}, u32[]{:S(2)}, u32[]{:S(2)}) %all-to-all-start.2) | async-done | bytes 327712 | tf_op jit(solution)/shard_map/all_to_all | solution.py:387
  95.4 1.2 broadcast_in_dim.20
  96.6 5.0 %all-to-all-start.3 = ((f32[4,64,1280]{2,1,0:T(8,128)}), f32[4,64,1280]{2,1,0:T(8,128)S(1)}, u32[]{:S(2)}, u32[]{:S(2)}) async-start(f32[4,64,1280]{2,1,0:T(8,128)} %broadcast_in_dim.20), calls=%async_computation.3 | async-start | bytes 2621440 | tf_op jit(solution)/shard_map/all_to_all | solution.py:387
  101.5 0.0 collective-permute-start.14
  101.5 1.3 %collective-permute-done.14.other_ref = f32[128,256]{1,0:T(8,128)S(1)} collective-permute-done((f32[128,256]{1,0:T(8,128)S(1)}, f32[128,256]{1,0:T(8,128)S(1)}, u32[]{:S(2)}, u32[]{:S(2)}) %collective-permute-start.14) | collective-permute-done | bytes 131104 | tf_op jit(solution)/shard_map/ppermute | solution.py:56
  102.9 6.6 %factor_first.1 = (f32[128,128]{1,0:T(8,128)S(1)}, f32[128,128]{1,0:T(8,128)S(1)}, f32[128,128]{1,0:T(8,128)S(1)}) custom-call(s32[1]{0:T(128)} %bitcast.x_ref, s32[1]{0:T(128)} %bitcast.1.y_ref, s32[1]{0:T(128)} %bitcast.2.core_ref, f32[128,256]{1,0:T(8,128)S(1)} %constant_dynamic-update-slice_fusion.mine_ref, f32[128,256]{1,0:T(8,128)S(1)} %collective-permute-done.14.other_ref), custom_call_target="tpu_custom_call" | custom-call | tf_op jit(solution)/shard_map/factor_first/pallas_call | solution.py:312
  109.5 7.8 %factor_last.1 = (f32[256,256]{1,0:T(8,128)S(1)}, bf16[1024,768]{1,0:T(8,128)(2,1)S(1)}) custom-call(f32[128,128]{1,0:T(8,128)S(1)} %get-tuple-element.19.w11_ref, f32[128,128]{1,0:T(8,128)S(1)} %get-tuple-element.20.l_ref, f32[128,128]{1,0:T(8,128)S(1)} %get-tuple-element.21.s_ref, f32[1024,256]{1,0:T(8,128)} %copy-done), custom_call_target="tpu_custom_call" | custom-call | tf_op jit(solution)/shard_map/factor_last/pallas_call | solution.py:325
  117.2 0.0 all-to-all-done.3
  117.3 5.4 %update.1 = (f32[10,1024,128]{2,1,0:T(8,128)}, f32[10,256,128]{2,1,0:T(8,128)}) custom-call(f32[256,256]{1,0:T(8,128)S(1)} %get-tuple-element.23.w_ref, bf16[1024,768]{1,0:T(8,128)(2,1)S(1)} %get-tuple-element.24.q_ref, f32[256,1280]{1,0:T(8,128)S(1)} %bitcast.17, f32[10,1024,128]{2,1,0:T(8,128)} %bitcast.22), custom_call_target="tpu_custom_call" | custom-call | tf_op jit(solution)/shard_map/update/pallas_call | solution.py:369
  (9 shorter events, 0.0 us)
Async XLA Ops:
  1.7 11.4 %collective-permute-start.4 = (f32[512,128]{1,0:T(8,128)S(1)}, f32[512,128]{1,0:T(8,128)S(1)}, u32[]{:S(2)}, u32[]{:S(2)}) collective-permute-start(f32[512,128]{1,0:T(8,128)S(1)} %get-tuple-element.30), channel_id=1, source_target_pairs={{0,6},{1,7},{8,14},{9,15},{16,22},{17,23},{24,30},{25,31},{32,38},... | collective-permute-start | bytes 786440 | tf_op jit(solution)/shard_map/ppermute | solution.py:64
  6.4 8.0 %collective-permute-start = (f32[512,128]{1,0:T(8,128)S(1)}, f32[512,128]{1,0:T(8,128)S(1)}, u32[]{:S(2)}, u32[]{:S(2)}) collective-permute-start(f32[512,128]{1,0:T(8,128)S(1)} %get-tuple-element.31), channel_id=1, source_target_pairs={{0,2},{1,3},{8,10},{9,11},{16,18},{17,19},{24,26},{25,27},{32,34},... | collective-permute-start | bytes 786440 | tf_op jit(solution)/shard_map/ppermute | solution.py:63
  7.7 11.1 %collective-permute-start.3 = (f32[512,128]{1,0:T(8,128)S(1)}, f32[512,128]{1,0:T(8,128)S(1)}, u32[]{:S(2)}, u32[]{:S(2)}) collective-permute-start(f32[512,128]{1,0:T(8,128)S(1)} %get-tuple-element.30), channel_id=1, source_target_pairs={{0,2},{1,3},{8,10},{9,11},{16,18},{17,19},{24,26},{25,27},{32,34},... | collective-permute-start | bytes 786440 | tf_op jit(solution)/shard_map/ppermute | solution.py:65
  9.0 9.8 %collective-permute-start.2 = (f32[512,128]{1,0:T(8,128)S(1)}, f32[512,128]{1,0:T(8,128)S(1)}, u32[]{:S(2)}, u32[]{:S(2)}) collective-permute-start(f32[512,128]{1,0:T(8,128)S(1)} %get-tuple-element.31), channel_id=1, source_target_pairs={{0,6},{1,7},{8,14},{9,15},{16,22},{17,23},{24,30},{25,31},{32,38},... | collective-permute-start | bytes 786440 | tf_op jit(solution)/shard_map/ppermute | solution.py:66
  13.1 5.8 %collective-permute-start.5 = (f32[512,128]{1,0:T(8,128)S(1)}, f32[512,128]{1,0:T(8,128)S(1)}, u32[]{:S(2)}, u32[]{:S(2)}) collective-permute-start(f32[512,128]{1,0:T(8,128)S(1)} %collective-permute-done.4), channel_id=1, source_target_pairs={{6,4},{7,5},{14,12},{15,13},{22,20},{23,21},{30,28},{31,29},{38,36... | collective-permute-start | bytes 786440 | tf_op jit(solution)/shard_map/ppermute | solution.py:68
  14.4 4.5 %collective-permute-start.1 = (f32[512,128]{1,0:T(8,128)S(1)}, f32[512,128]{1,0:T(8,128)S(1)}, u32[]{:S(2)}, u32[]{:S(2)}) collective-permute-start(f32[512,128]{1,0:T(8,128)S(1)} %collective-permute-done), channel_id=1, source_target_pairs={{2,4},{3,5},{10,12},{11,13},{18,20},{19,21},{26,28},{27,29},{34,36... | collective-permute-start | bytes 786440 | tf_op jit(solution)/shard_map/ppermute | solution.py:67
  20.0 1.6 %collective-permute-start.7 = (f32[512,128]{1,0:T(8,128)S(1)}, f32[512,128]{1,0:T(8,128)S(1)}, u32[]{:S(2)}, u32[]{:S(2)}) collective-permute-start(f32[512,128]{1,0:T(8,128)S(1)} %get-tuple-element.28.mh_ref), channel_id=1, source_target_pairs={{0,1},{1,0},{2,3},{3,2},{4,5},{5,4},{6,7},{7,6},{8,9},{9,8},{10,11... | collective-permute-start | bytes 786440 | tf_op jit(solution)/shard_map/ppermute | solution.py:56
  20.1 1.9 %collective-permute-start.6 = (f32[512,128]{1,0:T(8,128)S(1)}, f32[512,128]{1,0:T(8,128)S(1)}, u32[]{:S(2)}, u32[]{:S(2)}) collective-permute-start(f32[512,128]{1,0:T(8,128)S(1)} %get-tuple-element.29.ml_ref), channel_id=1, source_target_pairs={{0,1},{1,0},{2,3},{3,2},{4,5},{5,4},{6,7},{7,6},{8,9},{9,8},{10,11... | collective-permute-start | bytes 786440 | tf_op jit(solution)/shard_map/ppermute | solution.py:56
  27.0 22.9 %copy-start = (f32[1024,256]{1,0:T(8,128)}, f32[1024,256]{1,0:T(8,128)S(1)}, u32[]{:S(2)}) copy-start(f32[1024,256]{1,0:T(8,128)S(1)} %get-tuple-element.22.p_hbm) | copy-start | bytes 3145732
  72.5 11.8 %collective-permute-start.10 = (f32[8,256]{1,0:T(8,128)S(1)}, f32[8,256]{1,0:T(8,128)S(1)}, u32[]{:S(2)}, u32[]{:S(2)}) collective-permute-start(f32[8,256]{1,0:T(8,128)S(1)} %gram_z.1), channel_id=1, source_target_pairs={{0,2},{2,4},{4,6},{6,0},{1,3},{3,5},{5,7},{7,1},{8,10},{10,12},{12... | collective-permute-start | bytes 24584 | tf_op jit(solution)/shard_map/ppermute | solution.py:203
  75.7 8.6 %collective-permute-start.9 = (f32[8,256]{1,0:T(8,128)S(1)}, f32[8,256]{1,0:T(8,128)S(1)}, u32[]{:S(2)}, u32[]{:S(2)}) collective-permute-start(f32[8,256]{1,0:T(8,128)S(1)} %gram_z.1), channel_id=1, source_target_pairs={{0,4},{2,6},{4,0},{6,2},{1,5},{3,7},{5,1},{7,3},{8,12},{10,14},{12... | collective-permute-start | bytes 24584 | tf_op jit(solution)/shard_map/ppermute | solution.py:203
  78.3 6.0 %collective-permute-start.8 = (f32[8,256]{1,0:T(8,128)S(1)}, f32[8,256]{1,0:T(8,128)S(1)}, u32[]{:S(2)}, u32[]{:S(2)}) collective-permute-start(f32[8,256]{1,0:T(8,128)S(1)} %gram_z.1), channel_id=1, source_target_pairs={{0,6},{2,0},{4,2},{6,4},{1,7},{3,1},{5,3},{7,5},{8,14},{10,8},{12,... | collective-permute-start | bytes 24584 | tf_op jit(solution)/shard_map/ppermute | solution.py:203
  80.9 14.5 %all-to-all-start.2 = ((f32[8,8,1280]{2,1,0:T(8,128)}), f32[8,8,1280]{2,1,0:T(8,128)S(1)}, u32[]{:S(2)}, u32[]{:S(2)}) async-start(f32[8,8,1280]{2,1,0:T(8,128)} %copies_z.1), calls=%async_computation.2 | async-start | bytes 655360 | tf_op jit(solution)/shard_map/all_to_all | solution.py:387
  84.4 7.5 %collective-permute-start.13 = (f32[32,256]{1,0:T(8,128)S(1)}, f32[32,256]{1,0:T(8,128)S(1)}, u32[]{:S(2)}, u32[]{:S(2)}) collective-permute-start(f32[32,256]{1,0:T(8,128)S(1)} %pad_maximum_fusion), channel_id=1, source_target_pairs={{0,8},{8,16},{16,24},{24,0},{1,9},{9,17},{17,25},{25,1},{2,10},{10... | collective-permute-start | bytes 98312 | tf_op jit(solution)/shard_map/ppermute | solution.py:203
  84.7 7.2 %collective-permute-start.12 = (f32[32,256]{1,0:T(8,128)S(1)}, f32[32,256]{1,0:T(8,128)S(1)}, u32[]{:S(2)}, u32[]{:S(2)}) collective-permute-start(f32[32,256]{1,0:T(8,128)S(1)} %pad_maximum_fusion), channel_id=1, source_target_pairs={{0,16},{8,24},{16,0},{24,8},{1,17},{9,25},{17,1},{25,9},{2,18},{10... | collective-permute-start | bytes 98312 | tf_op jit(solution)/shard_map/ppermute | solution.py:203
  88.0 3.9 %collective-permute-start.11 = (f32[32,256]{1,0:T(8,128)S(1)}, f32[32,256]{1,0:T(8,128)S(1)}, u32[]{:S(2)}, u32[]{:S(2)}) collective-permute-start(f32[32,256]{1,0:T(8,128)S(1)} %pad_maximum_fusion), channel_id=1, source_target_pairs={{0,24},{8,0},{16,8},{24,16},{1,25},{9,1},{17,9},{25,17},{2,26},{10... | collective-permute-start | bytes 98312 | tf_op jit(solution)/shard_map/ppermute | solution.py:203
  96.6 20.7 %all-to-all-start.3 = ((f32[4,64,1280]{2,1,0:T(8,128)}), f32[4,64,1280]{2,1,0:T(8,128)S(1)}, u32[]{:S(2)}, u32[]{:S(2)}) async-start(f32[4,64,1280]{2,1,0:T(8,128)} %broadcast_in_dim.20), calls=%async_computation.3 | async-start | bytes 2621440 | tf_op jit(solution)/shard_map/all_to_all | solution.py:387
  101.5 1.3 %collective-permute-start.14 = (f32[128,256]{1,0:T(8,128)S(1)}, f32[128,256]{1,0:T(8,128)S(1)}, u32[]{:S(2)}, u32[]{:S(2)}) collective-permute-start(f32[128,256]{1,0:T(8,128)S(1)} %constant_dynamic-update-slice_fusion.mine_ref), channel_id=1, source_target_pairs={{0,1},{1,0},{2,3},{3,2},{4,5},{5,4},{6,7},{7,6},{8,9},{9,8},{10,11... | collective-permute-start | bytes 393224 | tf_op jit(solution)/shard_map/ppermute | solution.py:56
